TPU v7x, 32 devices: a whole 2x2x4 slice. The times are simulated.
32 devices in a mesh: blk: 4 (over z), seq: 2 (over y), shard: 4 (over x, core).
Axes of the slice: x: 2, y: 2, z: 4, core: 2. Of those that a mesh axis runs over, the one named last changes fastest.
Arguments:
- tokens: bfloat16 [8, 2048, 768], P(('seq', 'shard'), 'blk'), may hold values from -6 to 6
- segments: int32 [8, 2048], P(('seq', 'shard')), may hold values from 0 to 2047, as said below
- live_mask: int32 [8, 2048], P(('seq', 'shard')), may hold values from 0 to 1, as said below
- query_weight: bfloat16 [768, 768], P(('seq', 'shard')), may hold values from -0.21875 to 0.21875
- key_weight: bfloat16 [768, 768], P(('seq', 'shard')), may hold values from -0.21875 to 0.21875
- value_weight: bfloat16 [768, 768], P(('seq', 'shard')), may hold values from -0.21875 to 0.21875
- out_weight: bfloat16 [768, 768], P(('seq', 'shard')), may hold values from -6 to 6
- query_bias: bfloat16 [768], P(('seq', 'shard')), may hold values from -1 to 1
- value_bias: bfloat16 [768], P(('seq', 'shard')), may hold values from -1 to 1
- out_bias: bfloat16 [768], P(('seq', 'shard')), may hold values from -1 to 1
- first_gain: bfloat16 [768], P(('seq', 'shard')), may hold values from 0.5 to 1.5
- first_shift: bfloat16 [768], P(('seq', 'shard')), may hold values from -1 to 1
- up_weight: bfloat16 [768, 3072], P(('seq', 'shard')), may hold values from -0.21875 to 0.21875
- up_bias: bfloat16 [3072], P(('seq', 'shard')), may hold values from -1 to 1
- down_weight: bfloat16 [3072, 768], P(('seq', 'shard')), may hold values from -0.109375 to 0.109375
- down_bias: bfloat16 [768], P(('seq', 'shard')), may hold values from -1 to 1
- second_gain: bfloat16 [768], P(('seq', 'shard')), may hold values from 0.5 to 1.5
- second_shift: bfloat16 [768], P(('seq', 'shard')), may hold values from -1 to 1
- cotangent: bfloat16 [8, 2048, 768], P(('seq', 'shard'), 'blk'), may hold values from -6 to 6
Outputs:
- layer_out: bfloat16 [8, 2048, 768], P(('seq', 'shard'), 'blk')
- token_grad: bfloat16 [8, 2048, 768], P(('seq', 'shard'), 'blk')
- query_weight_grad: float32 [768, 768], P(('seq', 'shard'))
- key_weight_grad: float32 [768, 768], P(('seq', 'shard'))
- value_weight_grad: float32 [768, 768], P(('seq', 'shard'))
- out_weight_grad: float32 [768, 768], P(('seq', 'shard'))
- query_bias_grad: float32 [768], P(('seq', 'shard'))
- value_bias_grad: float32 [768], P(('seq', 'shard'))
- out_bias_grad: float32 [768], P(('seq', 'shard'))
- first_gain_grad: float32 [768], P(('seq', 'shard'))
- first_shift_grad: float32 [768], P(('seq', 'shard'))
- up_weight_grad: float32 [768, 3072], P(('seq', 'shard'))
- up_bias_grad: float32 [3072], P(('seq', 'shard'))
- down_weight_grad: float32 [3072, 768], P(('seq', 'shard'))
- down_bias_grad: float32 [768], P(('seq', 'shard'))
- second_gain_grad: float32 [768], P(('seq', 'shard'))
- second_shift_grad: float32 [768], P(('seq', 'shard'))
Inputs may be any that keep to these rules, and one draw needn't show every extreme that they name: `segments`: ids never fall along a sequence and start at 0; in at least one sequence one document begins within the first 512 tokens and ends within the last 512; the padding tokens form the sequence's last document, with id 2048 - 1. `live_mask`: each sequence ends with 1 to 256 padding tokens, marked 0; all others are 1.
All inputs are finite; a program needn't handle non-finite values.
Results may differ from a plain program's by a relative error of at most 0.02.
Values may be sent and summed in bfloat16 or wider, within the bound.
A program may use at most 128 MiB of HBM per device.

v0:
```python
import jax
import jax.numpy as jnp
from jax import lax
from jax.sharding import PartitionSpec as P

HEAD_DIM = 64


EPSILON = 1e-06
MASKED = -1e30


def shifted(value, axis, steps):
    count = lax.axis_size(axis)
    pairs = [(source, (source + steps) % count) for source in range(count)]
    return lax.ppermute(value, axis, pairs)


def normalize(hidden, gain, shift):
    center = hidden - jnp.mean(hidden, axis=-1, keepdims=True)
    spread = jnp.mean(center * center, axis=-1, keepdims=True)
    return center * lax.rsqrt(spread + EPSILON) * gain + shift


def smooth_gate(hidden):
    return jax.nn.gelu(hidden, approximate=False)


def contract_rows(left, right):
    return lax.dot_general(
        left, right, (((0,), (0,)), ((), ())), preferred_element_type=jnp.float32
    )


def times_transpose(left, right):
    return lax.dot_general(
        left, right, (((1,), (1,)), ((), ())), preferred_element_type=jnp.float32
    )


def rotate_pair(pair):
    return shifted(pair, "blk", 1)


def rotate_grads(grads):
    return shifted(grads.astype(jnp.bfloat16), "blk", 1).astype(grads.dtype)


def per_device(
    tokens,
    segments,
    live_mask,
    query_weight,
    key_weight,
    value_weight,
    out_weight,
    query_bias,
    value_bias,
    out_bias,
    first_gain,
    first_shift,
    up_weight,
    up_bias,
    down_weight,
    down_bias,
    second_gain,
    second_shift,
    cotangent,
):
    (
        query_weight,
        key_weight,
        value_weight,
        out_weight,
        query_bias,
        value_bias,
        out_bias,
        first_gain,
        first_shift,
        up_weight,
        up_bias,
        down_weight,
        down_bias,
        second_gain,
        second_shift,
    ) = (
        lax.all_gather(query_weight, ("seq", "shard"), axis=0, tiled=True),
        lax.all_gather(key_weight, ("seq", "shard"), axis=0, tiled=True),
        lax.all_gather(value_weight, ("seq", "shard"), axis=0, tiled=True),
        lax.all_gather(out_weight, ("seq", "shard"), axis=0, tiled=True),
        lax.all_gather(query_bias, ("seq", "shard"), axis=0, tiled=True),
        lax.all_gather(value_bias, ("seq", "shard"), axis=0, tiled=True),
        lax.all_gather(out_bias, ("seq", "shard"), axis=0, tiled=True),
        lax.all_gather(first_gain, ("seq", "shard"), axis=0, tiled=True),
        lax.all_gather(first_shift, ("seq", "shard"), axis=0, tiled=True),
        lax.all_gather(up_weight, ("seq", "shard"), axis=0, tiled=True),
        lax.all_gather(up_bias, ("seq", "shard"), axis=0, tiled=True),
        lax.all_gather(down_weight, ("seq", "shard"), axis=0, tiled=True),
        lax.all_gather(down_bias, ("seq", "shard"), axis=0, tiled=True),
        lax.all_gather(second_gain, ("seq", "shard"), axis=0, tiled=True),
        lax.all_gather(second_shift, ("seq", "shard"), axis=0, tiled=True),
    )
    inputs = tokens[0]
    rows, width = inputs.shape
    heads = width // HEAD_DIM
    cycle_size = lax.axis_size("blk")
    place = lax.axis_index("blk")
    doc_ids = segments[0]
    live_all = live_mask[0]
    start = place * rows
    query_doc = lax.dynamic_slice_in_dim(doc_ids, start, rows)
    query_place = start + jnp.arange(rows, dtype=jnp.int32)
    scale = HEAD_DIM ** (-0.5)
    queries = (
        (
            jnp.dot(inputs, query_weight, preferred_element_type=jnp.float32)
            + query_bias.astype(jnp.float32)
        )
        * scale
    ).astype(jnp.bfloat16)
    key_rows = jnp.dot(inputs, key_weight, preferred_element_type=jnp.float32).astype(jnp.bfloat16)
    value_rows = (
        jnp.dot(inputs, value_weight, preferred_element_type=jnp.float32)
        + value_bias.astype(jnp.float32)
    ).astype(jnp.bfloat16)
    pair = jnp.stack([key_rows, value_rows])
    query_heads = queries.reshape(rows, heads, HEAD_DIM)

    def scores(key_block, block):
        key_start = block * rows
        key_doc = lax.dynamic_slice_in_dim(doc_ids, key_start, rows)
        key_live = lax.dynamic_slice_in_dim(live_all, key_start, rows)
        key_place = key_start + jnp.arange(rows, dtype=jnp.int32)
        mask = (query_doc[:, None] == key_doc[None, :]) & (
            (key_live[None, :] > 0) | (query_place[:, None] == key_place[None, :])
        )
        raw = jnp.einsum(
            "qhd,khd->hqk",
            query_heads,
            key_block.reshape(rows, heads, HEAD_DIM),
            preferred_element_type=jnp.float32,
        )
        return (raw, mask[None])

    def add_stats(stats, key_block, block):
        top, mass = stats
        raw, mask = scores(key_block, block)
        new_top = jnp.maximum(top, jnp.max(jnp.where(mask, raw, MASKED), axis=-1))
        terms = jnp.where(mask, jnp.exp(raw - new_top[:, :, None]), 0.0)
        return (new_top, mass * jnp.exp(top - new_top) + jnp.sum(terms, axis=-1))

    stats = (jnp.full((heads, rows), MASKED, jnp.float32), jnp.zeros((heads, rows), jnp.float32))

    def stat_step(step, carry):
        key_now, stats = carry
        stats = add_stats(stats, key_now, (place - step) % cycle_size)
        return (shifted(key_now, "blk", 1), stats)

    key_now, stats = lax.fori_loop(0, cycle_size - 1, stat_step, (key_rows, stats))
    stats = add_stats(stats, key_now, (place + 1) % cycle_size)
    log_mass = stats[0] + jnp.log(stats[1])

    def add_output(summed, block_pair, block):
        raw, mask = scores(block_pair[0], block)
        shares = jnp.where(mask, jnp.exp(raw - log_mass[:, :, None]), 0.0).astype(jnp.bfloat16)
        return summed + jnp.einsum(
            "hqk,khd->qhd",
            shares,
            block_pair[1].reshape(rows, heads, HEAD_DIM),
            preferred_element_type=jnp.float32,
        )

    summed = jnp.zeros((rows, heads, HEAD_DIM), jnp.float32)

    def out_step(step, carry):
        pair_now, summed = carry
        summed = add_output(summed, pair_now, (place - step) % cycle_size)
        return (rotate_pair(pair_now), summed)

    pair_now, summed = lax.fori_loop(0, cycle_size - 1, out_step, (pair, summed))
    summed = add_output(summed, pair_now, (place + 1) % cycle_size)
    attended = summed.reshape(rows, width).astype(jnp.bfloat16)
    first_sum = inputs.astype(jnp.float32) + (
        jnp.dot(attended, out_weight, preferred_element_type=jnp.float32)
        + out_bias.astype(jnp.float32)
    )
    first_norm, first_pull = jax.vjp(
        normalize, first_sum, first_gain.astype(jnp.float32), first_shift.astype(jnp.float32)
    )
    first_low = first_norm.astype(jnp.bfloat16)
    hidden = jnp.dot(first_low, up_weight, preferred_element_type=jnp.float32) + up_bias.astype(
        jnp.float32
    )
    gated, gate_pull = jax.vjp(smooth_gate, hidden)
    gated_low = gated.astype(jnp.bfloat16)
    second_sum = first_norm + (
        jnp.dot(gated_low, down_weight, preferred_element_type=jnp.float32)
        + down_bias.astype(jnp.float32)
    )
    result, second_pull = jax.vjp(
        normalize, second_sum, second_gain.astype(jnp.float32), second_shift.astype(jnp.float32)
    )
    second_grad, second_gain_grad, second_shift_grad = second_pull(cotangent[0].astype(jnp.float32))
    down_bias_grad = jnp.sum(second_grad, axis=0)
    second_low = second_grad.astype(jnp.bfloat16)
    down_weight_grad = contract_rows(gated_low, second_low)
    (hidden_grad,) = gate_pull(times_transpose(second_low, down_weight))
    up_bias_grad = jnp.sum(hidden_grad, axis=0)
    hidden_low = hidden_grad.astype(jnp.bfloat16)
    up_weight_grad = contract_rows(first_low, hidden_low)
    norm_grad = second_grad + times_transpose(hidden_low, up_weight)
    first_grad, first_gain_grad, first_shift_grad = first_pull(norm_grad)
    out_bias_grad = jnp.sum(first_grad, axis=0)
    first_grad_low = first_grad.astype(jnp.bfloat16)
    out_weight_grad = contract_rows(attended, first_grad_low)
    grad_heads = (
        times_transpose(first_grad_low, out_weight)
        .astype(jnp.bfloat16)
        .reshape(rows, heads, HEAD_DIM)
    )
    delta = jnp.einsum("qhd,qhd->hq", grad_heads.astype(jnp.float32), summed)

    def add_grads(block_pair, block):
        raw, mask = scores(block_pair[0], block)
        shares = jnp.where(mask, jnp.exp(raw - log_mass[:, :, None]), 0.0)
        key_heads = block_pair[0].reshape(rows, heads, HEAD_DIM)
        value_heads = block_pair[1].reshape(rows, heads, HEAD_DIM)
        value_part = jnp.einsum(
            "hqk,qhd->khd",
            shares.astype(jnp.bfloat16),
            grad_heads,
            preferred_element_type=jnp.float32,
        )
        share_grad = jnp.einsum(
            "qhd,khd->hqk", grad_heads, value_heads, preferred_element_type=jnp.float32
        )
        score_grad = (shares * (share_grad - delta[:, :, None])).astype(jnp.bfloat16)
        query_part = jnp.einsum(
            "hqk,khd->qhd", score_grad, key_heads, preferred_element_type=jnp.float32
        )
        key_part = jnp.einsum(
            "hqk,qhd->khd", score_grad, query_heads, preferred_element_type=jnp.float32
        )
        return (
            query_part,
            jnp.stack([key_part.reshape(rows, width), value_part.reshape(rows, width)]),
        )

    query_total = jnp.zeros((rows, heads, HEAD_DIM), jnp.float32)

    def grad_step(step, carry):
        pair_now, grad_now, query_total = carry
        query_part, pair_part = add_grads(pair_now, (place - step) % cycle_size)
        return (rotate_pair(pair_now), rotate_grads(grad_now + pair_part), query_total + query_part)

    pair_now, grad_now, query_total = lax.fori_loop(
        0, cycle_size - 1, grad_step, (pair, jnp.zeros((2, rows, width), jnp.float32), query_total)
    )
    query_part, pair_part = add_grads(pair_now, (place + 1) % cycle_size)
    query_total = query_total + query_part
    pair_grad = rotate_grads(grad_now + pair_part)
    query_pre = query_total.reshape(rows, width) * scale
    query_bias_grad = jnp.sum(query_pre, axis=0)
    value_bias_grad = jnp.sum(pair_grad[1], axis=0)
    query_low = query_pre.astype(jnp.bfloat16)
    key_low = pair_grad[0].astype(jnp.bfloat16)
    value_low = pair_grad[1].astype(jnp.bfloat16)
    query_weight_grad = contract_rows(inputs, query_low)
    key_weight_grad = contract_rows(inputs, key_low)
    value_weight_grad = contract_rows(inputs, value_low)
    token_grad = (
        first_grad
        + times_transpose(query_low, query_weight)
        + times_transpose(key_low, key_weight)
        + times_transpose(value_low, value_weight)
    )
    (
        part_a,
        part_b,
        part_c,
        part_d,
        part_e,
        part_f,
        part_g,
        part_h,
        part_i,
        part_j,
        part_k,
        part_l,
        part_m,
        part_n,
        part_o,
    ) = (
        lax.psum_scatter(
            query_weight_grad.astype(jnp.bfloat16),
            ("seq", "shard"),
            scatter_dimension=0,
            tiled=True,
        ).astype(jnp.float32),
        lax.psum_scatter(
            key_weight_grad.astype(jnp.bfloat16), ("seq", "shard"), scatter_dimension=0, tiled=True
        ).astype(jnp.float32),
        lax.psum_scatter(
            value_weight_grad.astype(jnp.bfloat16),
            ("seq", "shard"),
            scatter_dimension=0,
            tiled=True,
        ).astype(jnp.float32),
        lax.psum_scatter(
            out_weight_grad.astype(jnp.bfloat16), ("seq", "shard"), scatter_dimension=0, tiled=True
        ).astype(jnp.float32),
        lax.psum_scatter(
            query_bias_grad.astype(jnp.bfloat16), ("seq", "shard"), scatter_dimension=0, tiled=True
        ).astype(jnp.float32),
        lax.psum_scatter(
            value_bias_grad.astype(jnp.bfloat16), ("seq", "shard"), scatter_dimension=0, tiled=True
        ).astype(jnp.float32),
        lax.psum_scatter(
            out_bias_grad.astype(jnp.bfloat16), ("seq", "shard"), scatter_dimension=0, tiled=True
        ).astype(jnp.float32),
        lax.psum_scatter(
            first_gain_grad.astype(jnp.bfloat16), ("seq", "shard"), scatter_dimension=0, tiled=True
        ).astype(jnp.float32),
        lax.psum_scatter(
            first_shift_grad.astype(jnp.bfloat16), ("seq", "shard"), scatter_dimension=0, tiled=True
        ).astype(jnp.float32),
        lax.psum_scatter(
            up_weight_grad.astype(jnp.bfloat16), ("seq", "shard"), scatter_dimension=0, tiled=True
        ).astype(jnp.float32),
        lax.psum_scatter(
            up_bias_grad.astype(jnp.bfloat16), ("seq", "shard"), scatter_dimension=0, tiled=True
        ).astype(jnp.float32),
        lax.psum_scatter(
            down_weight_grad.astype(jnp.bfloat16), ("seq", "shard"), scatter_dimension=0, tiled=True
        ).astype(jnp.float32),
        lax.psum_scatter(
            down_bias_grad.astype(jnp.bfloat16), ("seq", "shard"), scatter_dimension=0, tiled=True
        ).astype(jnp.float32),
        lax.psum_scatter(
            second_gain_grad.astype(jnp.bfloat16), ("seq", "shard"), scatter_dimension=0, tiled=True
        ).astype(jnp.float32),
        lax.psum_scatter(
            second_shift_grad.astype(jnp.bfloat16),
            ("seq", "shard"),
            scatter_dimension=0,
            tiled=True,
        ).astype(jnp.float32),
    )
    totals = (
        lax.psum(part_a.astype(jnp.bfloat16), "blk").astype(jnp.float32),
        lax.psum(part_b.astype(jnp.bfloat16), "blk").astype(jnp.float32),
        lax.psum(part_c.astype(jnp.bfloat16), "blk").astype(jnp.float32),
        lax.psum(part_d.astype(jnp.bfloat16), "blk").astype(jnp.float32),
        lax.psum(part_e.astype(jnp.bfloat16), "blk").astype(jnp.float32),
        lax.psum(part_f.astype(jnp.bfloat16), "blk").astype(jnp.float32),
        lax.psum(part_g.astype(jnp.bfloat16), "blk").astype(jnp.float32),
        lax.psum(part_h.astype(jnp.bfloat16), "blk").astype(jnp.float32),
        lax.psum(part_i.astype(jnp.bfloat16), "blk").astype(jnp.float32),
        lax.psum(part_j.astype(jnp.bfloat16), "blk").astype(jnp.float32),
        lax.psum(part_k.astype(jnp.bfloat16), "blk").astype(jnp.float32),
        lax.psum(part_l.astype(jnp.bfloat16), "blk").astype(jnp.float32),
        lax.psum(part_m.astype(jnp.bfloat16), "blk").astype(jnp.float32),
        lax.psum(part_n.astype(jnp.bfloat16), "blk").astype(jnp.float32),
        lax.psum(part_o.astype(jnp.bfloat16), "blk").astype(jnp.float32),
    )
    return (
        result.astype(jnp.bfloat16)[None],
        token_grad.astype(jnp.bfloat16)[None],
        totals[0],
        totals[1],
        totals[2],
        totals[3],
        totals[4],
        totals[5],
        totals[6],
        totals[7],
        totals[8],
        totals[9],
        totals[10],
        totals[11],
        totals[12],
        totals[13],
        totals[14],
    )


def solution(mesh):
    placed = (
        P(("seq", "shard"), "blk", None),
        P(("seq", "shard"), None),
        P(("seq", "shard"), None),
        P(("seq", "shard"), None),
        P(("seq", "shard"), None),
        P(("seq", "shard"), None),
        P(("seq", "shard"), None),
        P(("seq", "shard")),
        P(("seq", "shard")),
        P(("seq", "shard")),
        P(("seq", "shard")),
        P(("seq", "shard")),
        P(("seq", "shard"), None),
        P(("seq", "shard")),
        P(("seq", "shard"), None),
        P(("seq", "shard")),
        P(("seq", "shard")),
        P(("seq", "shard")),
        P(("seq", "shard"), "blk", None),
    )
    return jax.shard_map(
        per_device,
        mesh=mesh,
        in_specs=placed,
        out_specs=(
            P(("seq", "shard"), "blk", None),
            P(("seq", "shard"), "blk", None),
            P(("seq", "shard"), None),
            P(("seq", "shard"), None),
            P(("seq", "shard"), None),
            P(("seq", "shard"), None),
            P(("seq", "shard")),
            P(("seq", "shard")),
            P(("seq", "shard")),
            P(("seq", "shard")),
            P(("seq", "shard")),
            P(("seq", "shard"), None),
            P(("seq", "shard")),
            P(("seq", "shard"), None),
            P(("seq", "shard")),
            P(("seq", "shard")),
            P(("seq", "shard")),
        ),
        check_vma=False,
    )
```

profile of v0, /device:TPU:0, one launch (start us, length us, event | category | flops | bytes accessed | tf_op | source)
XLA Modules:
  0.0 988.6 jit_solution(12893083482036468027)
XLA Ops:
  19.2 25.7 %all-reduce.18 = (bf16[768]{0:T(1024)(128)(2,1)S(1)}, bf16[768]{0:T(1024)(128)(2,1)S(1)}, bf16[768]{0:T(1024)(128)(2,1)S(1)}, bf16[768]{0:T(1024)(128)(2,1)S(1)}...) all-reduce(bf16[768]{0:T(1024)(128)(2,1)S(1)} %dynamic-update-slice, ...), channel_id=1, replica_groups=mesh['blk'=4,'seq'=2,'shard'=4] {'seq','shard'}, use_global_device_ids=true, to_apply=%add | all-reduce | flops 5376 | bytes 21504
  45.6 7.8 all-gather
  55.8 2.4 convolution_convert_fusion.7
  58.5 4.3 all-gather.10.cloned.1.call-done
  68.3 2.8 copy.128
  71.1 17.7 %all-gather.12.cloned.1.call-done = bf16[768,768]{1,0:T(8,128)(2,1)} async-done(((bf16[96,768]{1,0:T(8,128)(2,1)}), bf16[768,768]{1,0:T(8,128)(2,1)}) %all-gather.12.cloned.1.call-update) | async-done | bytes 1179664 | tf_op jit(solution)/shard_map/all_gather | solution.py:87
  91.1 62.4 %while.58 = (s32[]{:T(128)}, bf16[512,768]{0,1:T(8,128)(2,1)S(1)}, f32[12,512]{1,0:T(8,128)S(1)}, f32[12,512]{1,0:T(8,128)S(1)}, s32[512]{0:T(512)S(1)}, /*index...) while((s32[]{:T(128)}, bf16[512,768]{0,1:T(8,128)(2,1)S(1)}, ...), condition=%wide.region_3.4_spmd.clone, body=%wide.region_0.3_spmd.clone.sunk | while | flops 419462688 | bytes 32583036 | solution.py:159
  97.5 15.3 %collective-permute-done = bf16[512,768]{0,1:T(8,128)(2,1)S(1)} collective-permute-done((bf16[512,768]{0,1:T(8,128)(2,1)S(1)}, bf16[512,768]{0,1:T(8,128)(2,1)S(1)}, u32[]{:S(2)}, u32[]{:S(2)}) %collective-permute-start) | collective-permute-done | bytes 786464 | tf_op jit(solution)/shard_map/while/body/eval_jaxpr/ppermute | solution.py:16
  117.7 15.9 %collective-permute-done = bf16[512,768]{0,1:T(8,128)(2,1)S(1)} collective-permute-done((bf16[512,768]{0,1:T(8,128)(2,1)S(1)}, bf16[512,768]{0,1:T(8,128)(2,1)S(1)}, u32[]{:S(2)}, u32[]{:S(2)}) %collective-permute-start) | collective-permute-done | bytes 786464 | tf_op jit(solution)/shard_map/while/body/eval_jaxpr/ppermute | solution.py:16
  138.5 15.0 %collective-permute-done = bf16[512,768]{0,1:T(8,128)(2,1)S(1)} collective-permute-done((bf16[512,768]{0,1:T(8,128)(2,1)S(1)}, bf16[512,768]{0,1:T(8,128)(2,1)S(1)}, u32[]{:S(2)}, u32[]{:S(2)}) %collective-permute-start) | collective-permute-done | bytes 786464 | tf_op jit(solution)/shard_map/while/body/eval_jaxpr/ppermute | solution.py:16
  157.7 109.1 %while.59 = (s32[]{:T(128)}, bf16[2,512,768]{1,2,0:T(8,128)(2,1)}, f32[512,12,64]{0,2,1:T(8,128)}, s32[512]{0:T(512)S(1)}, s32[]{:T(128)}, /*index=5*/s32[2048]{...) while((s32[]{:T(128)}, bf16[2,512,768]{1,2,0:T(8,128)(2,1)}, ...), condition=%wide.region_7.8_spmd.clone, body=%wide.region_6.7_spmd.clone.sunk | while | flops 816580096 | bytes 18656636 | solution.py:180
  160.8 6.8 bitcast_add_fusion.6
  167.6 27.5 %collective-permute-done.1 = bf16[2,512,768]{1,2,0:T(8,128)(2,1)} collective-permute-done((bf16[2,512,768]{1,2,0:T(8,128)(2,1)S(1)}, bf16[2,512,768]{1,2,0:T(8,128)(2,1)}, u32[]{:S(2)}, u32[]{:S(2)}) %collective-permute-start.1) | collective-permute-done | bytes 1572896 | tf_op jit(solution)/shard_map/while/body/eval_jaxpr/ppermute | solution.py:16
  198.0 7.3 bitcast_add_fusion.6
  205.4 26.1 %collective-permute-done.1 = bf16[2,512,768]{1,2,0:T(8,128)(2,1)} collective-permute-done((bf16[2,512,768]{1,2,0:T(8,128)(2,1)S(1)}, bf16[2,512,768]{1,2,0:T(8,128)(2,1)}, u32[]{:S(2)}, u32[]{:S(2)}) %collective-permute-start.1) | collective-permute-done | bytes 1572896 | tf_op jit(solution)/shard_map/while/body/eval_jaxpr/ppermute | solution.py:16
  234.3 7.3 bitcast_add_fusion.6
  241.7 25.1 %collective-permute-done.1 = bf16[2,512,768]{1,2,0:T(8,128)(2,1)} collective-permute-done((bf16[2,512,768]{1,2,0:T(8,128)(2,1)S(1)}, bf16[2,512,768]{1,2,0:T(8,128)(2,1)}, u32[]{:S(2)}, u32[]{:S(2)}) %collective-permute-start.1) | collective-permute-done | bytes 1572896 | tf_op jit(solution)/shard_map/while/body/eval_jaxpr/ppermute | solution.py:16
  266.8 2.4 fusion.88
  269.2 6.4 fusion.90
  275.6 2.4 fusion.91
  278.4 19.9 %multiply_convert_fusion.2 = (bf16[512,3072]{1,0:T(8,128)(2,1)}, f32[512,3072]{1,0:T(8,128)}, f32[512,3072]{1,0:T(8,128)}) fusion(f32[3072]{0:T(1024)S(1)} %bitcast.211, bf16[768,3072]{1,0:T(8,128)(2,1)} %all-gather.16.cloned.1.call-done, f32[512,768]{1,0:T(8,128)S(1)} %get-tuple-element.1222, f32[768]{0:T(1024)S(1)} %convert_element_type.303, ...), kind=kOutput, calls=%fused_computation.50 | convolution fusion | flops 2521694208 | bytes 22042624 | tf_op jit(solution)/shard_map/dot_general | solution.py:191
  298.3 6.1 fusion.92
  307.3 9.9 %fusion.93 = (bf16[3072]{0:T(1024)(128)(2,1)}, bf16[512,3072]{1,0:T(8,128)(2,1)}) fusion(f32[512,3072]{1,0:T(8,128)} %get-tuple-element.1200, bf16[3072,768]{1,0:T(8,128)(2,1)S(1)} %copy-done.49, f32[512,768]{1,0:T(8,128)S(1)} %get-tuple-element.1198, f32[512]{0:T(512)S(1)} %negate_multiply_fusion.2, f32[512,3072]{1,0:T(8,128)} %get-tuple-element.1223, ...), kind=kOutput, calls=%fused_computation.165 | convolution fusion | flops 2441868288 | bytes 22040576 | tf_op jit(solution)/shard_map/dot_general | solution.py:36
  317.3 5.6 multiply_reduce_fusion
  328.2 257.7 %while.60 = (s32[]{:T(128)}, bf16[2,512,768]{1,2,0:T(8,128)(2,1)}, f32[2,512,768]{1,2,0:T(8,128)}, f32[512,12,64]{0,2,1:T(8,128)}, s32[512]{0:T(512)S(1)}, /*ind...) while((s32[]{:T(128)}, bf16[2,512,768]{1,2,0:T(8,128)(2,1)}, ...), condition=%wide.region_17.18_spmd.clone, body=%wide.region_16.17_spmd.clone.sunk | while | flops 2044200448 | bytes 141651472 | solution.py:256
  333.5 3.4 fusion.188
  336.9 5.3 multiply_convert_fusion.5
  348.4 5.9 bitcast_add_fusion.7
  354.4 33.5 %collective-permute-done.3 = bf16[2,512,768]{1,2,0:T(8,128)(2,1)} collective-permute-done((bf16[2,512,768]{1,2,0:T(8,128)(2,1)}, bf16[2,512,768]{1,2,0:T(8,128)(2,1)}, u32[]{:S(2)}, u32[]{:S(2)}) %collective-permute-start.3) | collective-permute-done | bytes 1572896 | tf_op jit(solution)/shard_map/while/body/eval_jaxpr/ppermute | solution.py:16
  387.9 3.5 convert_element_type.456
  391.4 24.0 %collective-permute-done.2 = bf16[2,512,768]{1,2,0:T(8,128)(2,1)} collective-permute-done((bf16[2,512,768]{1,2,0:T(8,128)(2,1)S(1)}, bf16[2,512,768]{1,2,0:T(8,128)(2,1)}, u32[]{:S(2)}, u32[]{:S(2)}) %collective-permute-start.2) | collective-permute-done | bytes 1572896 | tf_op jit(solution)/shard_map/while/body/eval_jaxpr/ppermute | solution.py:16
  420.1 3.4 fusion.188
  423.5 5.3 multiply_convert_fusion.5
  435.1 6.4 bitcast_add_fusion.7
  441.5 33.1 %collective-permute-done.3 = bf16[2,512,768]{1,2,0:T(8,128)(2,1)} collective-permute-done((bf16[2,512,768]{1,2,0:T(8,128)(2,1)}, bf16[2,512,768]{1,2,0:T(8,128)(2,1)}, u32[]{:S(2)}, u32[]{:S(2)}) %collective-permute-start.3) | collective-permute-done | bytes 1572896 | tf_op jit(solution)/shard_map/while/body/eval_jaxpr/ppermute | solution.py:16
  474.5 3.5 convert_element_type.456
  478.1 23.0 %collective-permute-done.2 = bf16[2,512,768]{1,2,0:T(8,128)(2,1)} collective-permute-done((bf16[2,512,768]{1,2,0:T(8,128)(2,1)S(1)}, bf16[2,512,768]{1,2,0:T(8,128)(2,1)}, u32[]{:S(2)}, u32[]{:S(2)}) %collective-permute-start.2) | collective-permute-done | bytes 1572896 | tf_op jit(solution)/shard_map/while/body/eval_jaxpr/ppermute | solution.py:16
  505.9 3.4 fusion.188
  509.3 5.3 multiply_convert_fusion.5
  520.8 6.4 bitcast_add_fusion.7
  527.2 33.1 %collective-permute-done.3 = bf16[2,512,768]{1,2,0:T(8,128)(2,1)} collective-permute-done((bf16[2,512,768]{1,2,0:T(8,128)(2,1)}, bf16[2,512,768]{1,2,0:T(8,128)(2,1)}, u32[]{:S(2)}, u32[]{:S(2)}) %collective-permute-start.3) | collective-permute-done | bytes 1572896 | tf_op jit(solution)/shard_map/while/body/eval_jaxpr/ppermute | solution.py:16
  560.3 3.5 convert_element_type.456
  563.8 22.1 %collective-permute-done.2 = bf16[2,512,768]{1,2,0:T(8,128)(2,1)} collective-permute-done((bf16[2,512,768]{1,2,0:T(8,128)(2,1)S(1)}, bf16[2,512,768]{1,2,0:T(8,128)(2,1)}, u32[]{:S(2)}, u32[]{:S(2)}) %collective-permute-start.2) | collective-permute-done | bytes 1572896 | tf_op jit(solution)/shard_map/while/body/eval_jaxpr/ppermute | solution.py:16
  589.3 3.4 fusion.24
  592.7 7.3 multiply_convert_fusion.1
  600.1 4.9 fusion.98
  611.2 28.2 %collective-permute-done.4 = bf16[2,512,768]{1,2,0:T(8,128)(2,1)} collective-permute-done((bf16[2,512,768]{1,2,0:T(8,128)(2,1)}, bf16[2,512,768]{1,2,0:T(8,128)(2,1)}, u32[]{:S(2)}, u32[]{:S(2)}) %collective-permute-start.4) | collective-permute-done | bytes 1572896 | tf_op jit(solution)/shard_map/ppermute | solution.py:16
  641.2 2.9 fusion.54
  644.1 2.4 copy.103
  646.6 2.9 fusion.55
  649.5 2.4 copy.105
  652.0 3.6 convolution_convert_fusion.2
  655.7 7.5 convolution_convert_fusion.1
  663.8 7.3 convolution_convert_fusion
  675.8 13.2 %reduce-scatter.21.cloned.1.call-done = bf16[96,768]{1,0:T(8,128)(2,1)} async-done(((bf16[768,768]{1,0:T(8,128)(2,1)}), bf16[96,768]{1,0:T(8,128)(2,1)}) %reduce-scatter.21.cloned.1.call-update) | async-done | bytes 147472
  690.7 38.3 %reduce-scatter.23.cloned.1.call-done = bf16[96,768]{1,0:T(8,128)(2,1)} async-done(((bf16[768,768]{1,0:T(8,128)(2,1)}), bf16[96,768]{1,0:T(8,128)(2,1)}) %reduce-scatter.23.cloned.1.call-update) | async-done | bytes 147472
  730.8 39.1 %reduce-scatter.13.cloned.1.call-done = bf16[96,768]{1,0:T(8,128)(2,1)} async-done(((bf16[768,768]{1,0:T(8,128)(2,1)}), bf16[96,768]{1,0:T(8,128)(2,1)}) %reduce-scatter.13.cloned.1.call-update) | async-done | bytes 147472 | tf_op jit(solution)/shard_map/reduce_scatter | solution.py:309
  769.8 57.4 %reduce-scatter.15.cloned.1.call-done = bf16[96,3072]{1,0:T(8,128)(2,1)} async-done(((bf16[768,3072]{1,0:T(8,128)(2,1)}), bf16[96,3072]{1,0:T(8,128)(2,1)}) %reduce-scatter.15.cloned.1.call-update) | async-done | bytes 589840 | tf_op jit(solution)/shard_map/reduce_scatter | solution.py:327
  827.2 57.6 %reduce-scatter.17.cloned.1.call-done = bf16[384,768]{1,0:T(8,128)(2,1)} async-done(((bf16[3072,768]{1,0:T(8,128)(2,1)}), bf16[384,768]{1,0:T(8,128)(2,1)}) %reduce-scatter.17.cloned.1.call-update) | async-done | bytes 589840 | tf_op jit(solution)/shard_map/reduce_scatter | solution.py:333
  888.1 3.5 fusion.97
  891.9 24.3 %all-reduce.17 = (bf16[768]{0:T(1024)(128)(2,1)S(1)}, bf16[768]{0:T(1024)(128)(2,1)S(1)}, bf16[768]{0:T(1024)(128)(2,1)S(1)}, bf16[768]{0:T(1024)(128)(2,1)S(1)}...) all-reduce(bf16[768]{0:T(1024)(128)(2,1)S(1)} %dynamic-update-slice, ...), channel_id=1, replica_groups=mesh['blk'=4,'seq'=2,'shard'=4] {'seq','shard'}, use_global_device_ids=true, to_apply=%add.7 | all-reduce | flops 9984 | bytes 39936
  916.9 12.7 %all-reduce.19 = (bf16[96]{0:T(256)(128)(2,1)S(1)}, bf16[96]{0:T(256)(128)(2,1)S(1)}, bf16[96]{0:T(256)(128)(2,1)S(1)}, bf16[96]{0:T(256)(128)(2,1)S(1)}, bf16[9...) all-reduce(bf16[96]{0:T(256)(128)(2,1)S(1)} %dynamic-slice.12, ...), channel_id=1, replica_groups=mesh['blk'=4,'seq'=2,'shard'=4] {'blk'}, use_global_device_ids=true, to_apply=%region_28.29 | all-reduce | flops 1152 | bytes 4608 | tf_op jit(solution)/shard_map/psum | solution.py:354
  934.3 2.8 fusion.60
  941.3 30.2 %all-reduce.23.cloned.1.call-done = (bf16[96,768]{0,1:T(8,128)(2,1)}, bf16[96,768]{0,1:T(8,128)(2,1)}, bf16[96,768]{0,1:T(8,128)(2,1)}, bf16[96,768]{1,0:T(8,128...) async-done(((bf16[96,768]{0,1:T(8,128)(2,1)}, bf16[96,768]{0,1:T(8,128)(2,1)}, bf16[96,768]{0,1:T(8,128)(2,1)}, bf16[96,768]{1,0:T(8,128)(2,1)}, ...) | async-done | bytes 1769488 | tf_op jit(solution)/shard_map/psum | solution.py:350
  (352 shorter events, 134.2 us)
Async XLA Ops:
  7.2 48.6 %all-gather.8.cloned.1.call-start = ((), (), s32[]{:S(2)}) async-start(), calls=%async_computation.6 | async-start | bytes 1327104 | tf_op jit(solution)/shard_map/all_gather | solution.py:88
  7.9 54.9 %all-gather.10.cloned.1.call-start = ((), (), s32[]{:S(2)}) async-start(), calls=%async_computation.7 | async-start | bytes 1327104 | tf_op jit(solution)/shard_map/all_gather | solution.py:89
  8.7 80.1 %all-gather.12.cloned.1.call-start = ((), (), s32[]{:S(2)}) async-start(), calls=%async_computation.8 | async-start | bytes 1327104 | tf_op jit(solution)/shard_map/all_gather | solution.py:87
  9.4 266.2 %all-gather.14.cloned.1.call-start = ((), (), s32[]{:S(2)}) async-start(), calls=%async_computation.9 | async-start | bytes 1327104 | tf_op jit(solution)/shard_map/all_gather | solution.py:90
  10.0 268.4 %all-gather.16.cloned.1.call-start = ((), (), s32[]{:S(2)}) async-start(), calls=%async_computation.10 | async-start | bytes 5308416 | tf_op jit(solution)/shard_map/all_gather | solution.py:96
  10.6 52.2 %copy-start.15 = (bf16[1,512,768]{2,1,0:T(8,128)(2,1)S(1)}, bf16[1,512,768]{2,1,0:T(8,128)(2,1)}, u32[]{:S(2)}) copy-start(bf16[1,512,768]{2,1,0:T(8,128)(2,1)} %param.25) | copy-start | bytes 2359300
  10.6 287.7 %all-gather.18.cloned.1.call-start = ((), (), s32[]{:S(2)}) async-start(), calls=%async_computation.11 | async-start | bytes 5308416 | tf_op jit(solution)/shard_map/all_gather | solution.py:98
  11.2 662.9 %reduce-scatter.19.cloned.1.call-start = ((), (), s32[]{:S(2)}) async-start(), calls=%async_computation.15 | async-start | bytes 1327104
  53.4 244.9 %copy-start.45 = (f32[768]{0:T(1024)}, f32[768]{0:T(1024)S(1)}, u32[]{:S(2)}) copy-start(f32[768]{0:T(1024)S(1)} %convert_element_type.303) | copy-start | bytes 9220
  53.4 269.5 %copy-start.37 = (f32[768]{0:T(1024)}, f32[768]{0:T(1024)S(1)}, u32[]{:S(2)}) copy-start(f32[768]{0:T(1024)S(1)} %convert_element_type.302) | copy-start | bytes 9220
  55.8 99.7 %copy-start.12 = (pred[512,512]{0,1:T(8,128)(4,1)}, pred[512,512]{0,1:T(8,128)(4,1)S(1)}, u32[]{:S(2)}) copy-start(pred[512,512]{0,1:T(8,128)(4,1)S(1)} %or_and_fusion.3) | copy-start | bytes 786436
  58.2 6.7 copy-start.19
  68.3 20.5 %copy-start.16 = (bf16[1,512,768]{2,1,0:T(8,128)(2,1)S(1)}, bf16[1,512,768]{2,1,0:T(8,128)(2,1)}, u32[]{:S(2)}) copy-start(bf16[1,512,768]{2,1,0:T(8,128)(2,1)} %param.25) | copy-start | bytes 2359300
  71.1 20.0 %copy-start.25 = (s32[1,2048]{1,0:T(1,128)S(1)}, s32[1,2048]{1,0:T(1,128)}, u32[]{:S(2)}) copy-start(s32[1,2048]{1,0:T(1,128)} %param.26) | copy-start | bytes 24580
  71.1 20.0 %copy-start.26 = (s32[1,2048]{1,0:T(1,128)S(1)}, s32[1,2048]{1,0:T(1,128)}, u32[]{:S(2)}) copy-start(s32[1,2048]{1,0:T(1,128)} %param.27) | copy-start | bytes 24580
  91.2 21.6 %collective-permute-start = (bf16[512,768]{0,1:T(8,128)(2,1)S(1)}, bf16[512,768]{0,1:T(8,128)(2,1)S(1)}, u32[]{:S(2)}, u32[]{:S(2)}) collective-permute-start(bf16[512,768]{0,1:T(8,128)(2,1)S(1)} %copy.120), channel_id=1, source_target_pairs={{0,8},{8,16},{16,24},{24,0},{1,9},{9,17},{17,25},{25,1},{2,10},{10... | collective-permute-start | bytes 2359304 | tf_op jit(solution)/shard_map/while/body/eval_jaxpr/ppermute | solution.py:16
  112.8 20.8 %collective-permute-start = (bf16[512,768]{0,1:T(8,128)(2,1)S(1)}, bf16[512,768]{0,1:T(8,128)(2,1)S(1)}, u32[]{:S(2)}, u32[]{:S(2)}) collective-permute-start(bf16[512,768]{0,1:T(8,128)(2,1)S(1)} %copy.120), channel_id=1, source_target_pairs={{0,8},{8,16},{16,24},{24,0},{1,9},{9,17},{17,25},{25,1},{2,10},{10... | collective-permute-start | bytes 2359304 | tf_op jit(solution)/shard_map/while/body/eval_jaxpr/ppermute | solution.py:16
  133.7 19.8 %collective-permute-start = (bf16[512,768]{0,1:T(8,128)(2,1)S(1)}, bf16[512,768]{0,1:T(8,128)(2,1)S(1)}, u32[]{:S(2)}, u32[]{:S(2)}) collective-permute-start(bf16[512,768]{0,1:T(8,128)(2,1)S(1)} %copy.120), channel_id=1, source_target_pairs={{0,8},{8,16},{16,24},{24,0},{1,9},{9,17},{17,25},{25,1},{2,10},{10... | collective-permute-start | bytes 2359304 | tf_op jit(solution)/shard_map/while/body/eval_jaxpr/ppermute | solution.py:16
  159.3 35.8 %collective-permute-start.1 = (bf16[2,512,768]{1,2,0:T(8,128)(2,1)S(1)}, bf16[2,512,768]{1,2,0:T(8,128)(2,1)}, u32[]{:S(2)}, u32[]{:S(2)}) collective-permute-start(bf16[2,512,768]{1,2,0:T(8,128)(2,1)S(1)} %copy.131), channel_id=1, source_target_pairs={{0,8},{8,16},{16,24},{24,0},{1,9},{9,17},{17,25},{25,1},{2,10},{10... | collective-permute-start | bytes 4718600 | tf_op jit(solution)/shard_map/while/body/eval_jaxpr/ppermute | solution.py:16
  196.5 34.9 %collective-permute-start.1 = (bf16[2,512,768]{1,2,0:T(8,128)(2,1)S(1)}, bf16[2,512,768]{1,2,0:T(8,128)(2,1)}, u32[]{:S(2)}, u32[]{:S(2)}) collective-permute-start(bf16[2,512,768]{1,2,0:T(8,128)(2,1)S(1)} %copy.131), channel_id=1, source_target_pairs={{0,8},{8,16},{16,24},{24,0},{1,9},{9,17},{17,25},{25,1},{2,10},{10... | collective-permute-start | bytes 4718600 | tf_op jit(solution)/shard_map/while/body/eval_jaxpr/ppermute | solution.py:16
  232.8 34.0 %collective-permute-start.1 = (bf16[2,512,768]{1,2,0:T(8,128)(2,1)S(1)}, bf16[2,512,768]{1,2,0:T(8,128)(2,1)}, u32[]{:S(2)}, u32[]{:S(2)}) collective-permute-start(bf16[2,512,768]{1,2,0:T(8,128)(2,1)S(1)} %copy.131), channel_id=1, source_target_pairs={{0,8},{8,16},{16,24},{24,0},{1,9},{9,17},{17,25},{25,1},{2,10},{10... | collective-permute-start | bytes 4718600 | tf_op jit(solution)/shard_map/while/body/eval_jaxpr/ppermute | solution.py:16
  269.2 6.4 copy-start.17
  278.0 44.9 %copy-start.11 = (f32[512,768]{1,0:T(8,128)}, f32[512,768]{1,0:T(8,128)S(1)}, u32[]{:S(2)}) copy-start(f32[512,768]{1,0:T(8,128)S(1)} %get-tuple-element.1222) | copy-start | bytes 4718596
  278.1 44.9 %copy-start.35 = (f32[512]{0:T(512)}, f32[512]{0:T(512)S(1)}, u32[]{:S(2)}) copy-start(f32[512]{0:T(512)S(1)} %broadcast_multiply_fusion.1) | copy-start | bytes 6148
  278.4 44.6 %copy-start.42 = (f32[512]{0:T(512)}, f32[512]{0:T(512)S(1)}, u32[]{:S(2)}) copy-start(f32[512]{0:T(512)S(1)} %fusion.73) | copy-start | bytes 6148
  298.3 6.5 copy-start.9
  298.3 6.5 copy-start.27
  306.1 11.2 %slice-start = ((s8[4718592]{0:T(1024)(128)(4,1)}), s8[4194304]{0:T(1024)(128)(4,1)S(1)}, s32[]{:S(2)}) async-start(s8[4718592]{0:T(1024)(128)(4,1)} %bitcast.214), calls=%async_computation.19 | async-start | bytes 8388608
  306.8 10.5 %copy-start.10 = (f32[512,768]{1,0:T(8,128)}, f32[512,768]{1,0:T(8,128)S(1)}, u32[]{:S(2)}) copy-start(f32[512,768]{1,0:T(8,128)S(1)} %get-tuple-element.1198) | copy-start | bytes 4718596
  306.8 10.5 %copy-start.40 = (f32[512]{0:T(512)}, f32[512]{0:T(512)S(1)}, u32[]{:S(2)}) copy-start(f32[512]{0:T(512)S(1)} %negate_multiply_fusion.2) | copy-start | bytes 6148
  307.3 9.9 %slice-start.1 = ((s8[4718592]{0:T(1024)(128)(4,1)}), s8[524288]{0:T(1024)(128)(4,1)S(1)}, s32[]{:S(2)}) async-start(s8[4718592]{0:T(1024)(128)(4,1)} %bitcast.214), calls=%async_computation.20 | async-start | bytes 1048576
  323.6 4.6 copy-start.33
  342.2 4.2 copy-start.1
  348.4 39.4 %collective-permute-start.3 = (bf16[2,512,768]{1,2,0:T(8,128)(2,1)}, bf16[2,512,768]{1,2,0:T(8,128)(2,1)}, u32[]{:S(2)}, u32[]{:S(2)}) collective-permute-start(bf16[2,512,768]{1,2,0:T(8,128)(2,1)} %fusion.190), channel_id=1, source_target_pairs={{0,8},{8,16},{16,24},{24,0},{1,9},{9,17},{17,25},{25,1},{2,10},{10... | collective-permute-start | bytes 4718600 | tf_op jit(solution)/shard_map/while/body/eval_jaxpr/ppermute | solution.py:16
  348.4 67.0 %collective-permute-start.2 = (bf16[2,512,768]{1,2,0:T(8,128)(2,1)S(1)}, bf16[2,512,768]{1,2,0:T(8,128)(2,1)}, u32[]{:S(2)}, u32[]{:S(2)}) collective-permute-start(bf16[2,512,768]{1,2,0:T(8,128)(2,1)S(1)} %copy.142), channel_id=1, source_target_pairs={{0,8},{8,16},{16,24},{24,0},{1,9},{9,17},{17,25},{25,1},{2,10},{10... | collective-permute-start | bytes 4718600 | tf_op jit(solution)/shard_map/while/body/eval_jaxpr/ppermute | solution.py:16
  428.9 4.2 copy-start.1
  435.1 39.4 %collective-permute-start.3 = (bf16[2,512,768]{1,2,0:T(8,128)(2,1)}, bf16[2,512,768]{1,2,0:T(8,128)(2,1)}, u32[]{:S(2)}, u32[]{:S(2)}) collective-permute-start(bf16[2,512,768]{1,2,0:T(8,128)(2,1)} %fusion.190), channel_id=1, source_target_pairs={{0,8},{8,16},{16,24},{24,0},{1,9},{9,17},{17,25},{25,1},{2,10},{10... | collective-permute-start | bytes 4718600 | tf_op jit(solution)/shard_map/while/body/eval_jaxpr/ppermute | solution.py:16
  435.1 66.0 %collective-permute-start.2 = (bf16[2,512,768]{1,2,0:T(8,128)(2,1)S(1)}, bf16[2,512,768]{1,2,0:T(8,128)(2,1)}, u32[]{:S(2)}, u32[]{:S(2)}) collective-permute-start(bf16[2,512,768]{1,2,0:T(8,128)(2,1)S(1)} %copy.142), channel_id=1, source_target_pairs={{0,8},{8,16},{16,24},{24,0},{1,9},{9,17},{17,25},{25,1},{2,10},{10... | collective-permute-start | bytes 4718600 | tf_op jit(solution)/shard_map/while/body/eval_jaxpr/ppermute | solution.py:16
  514.6 4.2 copy-start.1
  520.8 39.4 %collective-permute-start.3 = (bf16[2,512,768]{1,2,0:T(8,128)(2,1)}, bf16[2,512,768]{1,2,0:T(8,128)(2,1)}, u32[]{:S(2)}, u32[]{:S(2)}) collective-permute-start(bf16[2,512,768]{1,2,0:T(8,128)(2,1)} %fusion.190), channel_id=1, source_target_pairs={{0,8},{8,16},{16,24},{24,0},{1,9},{9,17},{17,25},{25,1},{2,10},{10... | collective-permute-start | bytes 4718600 | tf_op jit(solution)/shard_map/while/body/eval_jaxpr/ppermute | solution.py:16
  520.8 65.1 %collective-permute-start.2 = (bf16[2,512,768]{1,2,0:T(8,128)(2,1)S(1)}, bf16[2,512,768]{1,2,0:T(8,128)(2,1)}, u32[]{:S(2)}, u32[]{:S(2)}) collective-permute-start(bf16[2,512,768]{1,2,0:T(8,128)(2,1)S(1)} %copy.142), channel_id=1, source_target_pairs={{0,8},{8,16},{16,24},{24,0},{1,9},{9,17},{17,25},{25,1},{2,10},{10... | collective-permute-start | bytes 4718600 | tf_op jit(solution)/shard_map/while/body/eval_jaxpr/ppermute | solution.py:16
  600.1 4.9 copy-start.3
  600.1 5.1 copy-start.5
  608.8 30.5 %collective-permute-start.4 = (bf16[2,512,768]{1,2,0:T(8,128)(2,1)}, bf16[2,512,768]{1,2,0:T(8,128)(2,1)}, u32[]{:S(2)}, u32[]{:S(2)}) collective-permute-start(bf16[2,512,768]{1,2,0:T(8,128)(2,1)} %fusion.40), channel_id=1, source_target_pairs={{0,8},{8,16},{16,24},{24,0},{1,9},{9,17},{17,25},{25,1},{2,10},{10... | collective-permute-start | bytes 4718600 | tf_op jit(solution)/shard_map/ppermute | solution.py:16
  611.1 77.9 %reduce-scatter.21.cloned.1.call-start = ((), (), s32[]{:S(2)}) async-start(), calls=%async_computation.16 | async-start | bytes 1327104
  646.5 5.5 copy-start.34
  646.5 82.5 %reduce-scatter.23.cloned.1.call-start = ((), (), s32[]{:S(2)}) async-start(), calls=%async_computation.17 | async-start | bytes 1327104
  651.9 3.7 copy-start.43
  651.9 3.8 copy-start.46
  652.0 117.9 %reduce-scatter.13.cloned.1.call-start = ((), (), s32[]{:S(2)}) async-start(), calls=%async_computation.12 | async-start | bytes 1327104 | tf_op jit(solution)/shard_map/reduce_scatter | solution.py:309
  655.6 171.6 %reduce-scatter.15.cloned.1.call-start = ((), (), s32[]{:S(2)}) async-start(), calls=%async_computation.13 | async-start | bytes 5308416 | tf_op jit(solution)/shard_map/reduce_scatter | solution.py:327
  663.2 221.6 %reduce-scatter.17.cloned.1.call-start = ((), (), s32[]{:S(2)}) async-start(), calls=%async_computation.14 | async-start | bytes 5308416 | tf_op jit(solution)/shard_map/reduce_scatter | solution.py:333
  671.2 300.4 %all-reduce.23.cloned.1.call-start = ((), (), s32[]{:S(2)}) async-start(), calls=%async_computation.18 | async-start | bytes 3833856 | tf_op jit(solution)/shard_map/psum | solution.py:350
  886.5 5.4 copy-start.39
  886.5 5.4 copy-start.44
  886.5 5.4 copy-start.47
  886.5 5.4 copy-start.48
  886.5 47.8 %copy-start.28 = (f32[768]{0:T(1024)S(1)}, f32[768]{0:T(1024)}, u32[]{:S(2)}) copy-start(f32[768]{0:T(1024)} %convert_element_type.308) | copy-start | bytes 9220
  886.5 47.8 %copy-start.30 = (f32[512]{0:T(512)S(1)}, f32[512]{0:T(512)}, u32[]{:S(2)}) copy-start(f32[512]{0:T(512)} %copy-done.29) | copy-start | bytes 6148
  886.5 47.8 %copy-start.32 = (f32[512]{0:T(512)S(1)}, f32[512]{0:T(512)}, u32[]{:S(2)}) copy-start(f32[512]{0:T(512)} %copy-done.31) | copy-start | bytes 6148
  934.3 5.0 copy-start.8
  934.3 5.0 copy-start.20
  934.3 5.0 copy-start.22
  971.5 9.2 copy-start.24
  (22 other events, 55.8 us)
Sparse Core Ops, SparseCore 0:
  9.9 26.8 all-gather.7
  38.7 24.0 all-gather.9
  64.7 24.0 all-gather.11
  90.5 24.0 all-gather.13
  116.4 38.9 all-gather.15
  157.1 38.9 all-gather.17
  611.2 37.3 reduce-scatter.18
  652.2 36.7 reduce-scatter.20
  692.2 36.7 reduce-scatter.22
  733.0 36.7 reduce-scatter.12
  773.3 53.8 reduce-scatter.14
  830.9 53.8 reduce-scatter.16
  888.2 83.2 all-reduce.22
where the time goes:
time: 994 us; the launch traced here: 989 us
  waiting for transfers between devices  583 us (59%)
  matrix products  192 us (19%)
  blocking collectives  70.5 us (7%)
  local copies, waits for them, and re-layouts  64 us (6%)
  other arithmetic  57.7 us (6%)
  between operations  17 us (2%)
    ppermute x13, waiting for transfers between devices, shifted(): return lax.ppermute(value, axis, pairs)  322 us
    reduce_scatter x1, waiting for transfers between devices, per_device(): lax.psum_scatter(down_weight_grad.astype(jnp.bfloat16), ('seq', 'shard'),...  57.6 us
    reduce_scatter x1, waiting for transfers between devices, per_device(): lax.psum_scatter(up_weight_grad.astype(jnp.bfloat16), ('seq', 'shard'), s...  57.4 us
    unnamed x16, waiting for transfers between devices  55.3 us
    unnamed x2, blocking collectives  50 us
    reduce_scatter x1, waiting for transfers between devices, per_device(): lax.psum_scatter(out_weight_grad.astype(jnp.bfloat16), ('seq', 'shard'),...  39.1 us
    unnamed x141, local copies, waits for them, and re-layouts  33.8 us
    psum x1, waiting for transfers between devices, per_device(): lax.psum(part_a.astype(jnp.bfloat16), 'blk').astype(jnp.float32)  30.2 us
  transfers between devices with their start and end apart: 26, of which 21 were waited for; matrix products, arithmetic and copies ran while one was open for 19% of the time, Pallas kernels for 0%

commit v1 on v0

v1 whole, which is shorter than its diff:
```python
import functools
import jax
import jax.numpy as jnp
from jax import lax
from jax.experimental import pallas as pl
from jax.experimental.pallas import tpu as pltpu
from jax.sharding import PartitionSpec as P

MESH = pl.DeviceIdType.MESH
ANY = pl.BlockSpec(memory_space=pl.ANY)
VMEM_LIMIT = 56 << 20
VM = pl.BlockSpec(memory_space=pltpu.VMEM)


class Place:
    def __init__(self):
        b = lax.axis_index("blk")
        s = lax.axis_index("seq")
        h = lax.axis_index("shard")
        x = h // 2
        c = h % 2
        self.b, self.s, self.h, self.x, self.c = b, s, h, x, c
        self.X = (b, s, (1 - x) * 2 + c)
        self.Y = (b, 1 - s, h)
        self.C = (b, s, x * 2 + 1 - c)
        self.L = (b - 1, s, h)
        self.R = (b + 1, s, h)
        self.me = s * 4 + h
        self.xi = s * 4 + (1 - x) * 2 + c
        self.yi = (1 - s) * 4 + h
        self.di = (1 - s) * 4 + (1 - x) * 2 + c

    def z(self, j):
        return (j, self.s, self.h)


def enter(p, nb, plane, line):
    bar = pltpu.get_barrier_semaphore()
    count = 0
    if plane:
        for peer in (p.X, p.Y, p.C):
            pl.semaphore_signal(bar, inc=1, device_id=peer, device_id_type=MESH)
        count = count + 3
    if line == "near":
        @pl.when(p.b > 0)
        def _():
            pl.semaphore_signal(bar, inc=1, device_id=p.L, device_id_type=MESH)

        @pl.when(p.b < nb - 1)
        def _():
            pl.semaphore_signal(bar, inc=1, device_id=p.R, device_id_type=MESH)
        count = count + jnp.where(p.b > 0, 1, 0) + jnp.where(p.b < nb - 1, 1, 0)
    if line == "all":
        for j in range(nb):
            @pl.when(p.b != j)
            def _():
                pl.semaphore_signal(bar, inc=1, device_id=p.z(j), device_id_type=MESH)
        count = count + nb - 1
    pl.semaphore_wait(bar, count)


def rcopy(src, dst, ss, rs, dev):
    return pltpu.make_async_remote_copy(
        src_ref=src, dst_ref=dst, send_sem=ss, recv_sem=rs, device_id=dev, device_id_type=MESH
    )


class LineGather:
    def __init__(self, p, nb, own, out, ssem, rsem):
        self.p, self.nb, self.own, self.out, self.ssem, self.rsem = p, nb, own, out, ssem, rsem

    def _copies(self, t):
        p, nb = self.p, self.nb
        rb = p.b - t
        lb = p.b + t
        src_r = self.own if t == 0 else self.out.at[jnp.maximum(rb, 0)]
        src_l = self.own if t == 0 else self.out.at[jnp.minimum(lb, nb - 1)]
        right = rcopy(src_r, self.out.at[jnp.maximum(rb, 0)], self.ssem.at[0, t], self.rsem.at[0, t], p.R)
        left = rcopy(src_l, self.out.at[jnp.minimum(lb, nb - 1)], self.ssem.at[1, t], self.rsem.at[1, t], p.L)
        return right, left, (rb >= 0) & (p.b < nb - 1), (lb <= nb - 1) & (p.b > 0)

    def start(self, t):
        right, left, cr, cl = self._copies(t)
        pl.when(cr)(right.start)
        pl.when(cl)(left.start)

    def wait_recv(self, t):
        p, nb = self.p, self.nb
        right, left, _, _ = self._copies(t)
        pl.when(p.b - 1 - t >= 0)(right.wait_recv)
        pl.when(p.b + 1 + t <= nb - 1)(left.wait_recv)

    def wait_send(self, t):
        right, left, cr, cl = self._copies(t)
        pl.when(cr)(right.wait_send)
        pl.when(cl)(left.wait_send)


class PlaneGather:
    def __init__(self, p, own, out, ssem, rsem, lsem):
        self.p = p
        rows = own.shape[0]
        half = rows // 2
        lo, hi = pl.ds(0, half), pl.ds(half, half)
        o = out
        self.x = rcopy(own, o.at[p.me], ssem.at[0], rsem.at[0], p.X)
        self.y = rcopy(own, o.at[p.me], ssem.at[1], rsem.at[1], p.Y)
        self.c = rcopy(own, o.at[p.me], ssem.at[2], rsem.at[2], p.C)
        self.local = pltpu.make_async_copy(own, o.at[p.me], lsem)
        self.fx = rcopy(o.at[p.yi, hi], o.at[p.yi, hi], ssem.at[3], rsem.at[3], p.X)
        self.fy = rcopy(o.at[p.xi, lo], o.at[p.xi, lo], ssem.at[4], rsem.at[4], p.Y)
        self.cx = rcopy(o.at[p.xi], o.at[p.xi], ssem.at[5], rsem.at[5], p.C)
        self.cy = rcopy(o.at[p.yi], o.at[p.yi], ssem.at[6], rsem.at[6], p.C)
        self.cd0 = rcopy(o.at[p.di, lo], o.at[p.di, lo], ssem.at[7], rsem.at[7], p.C)
        self.cd1 = rcopy(o.at[p.di, hi], o.at[p.di, hi], ssem.at[8], rsem.at[8], p.C)

    def start(self):
        self.x.start(); self.y.start(); self.c.start(); self.local.start()

    def forward(self):
        self.x.wait_recv()
        self.fy.start()
        self.cx.start()
        self.y.wait_recv()
        self.fx.start()
        self.cy.start()

    def diag(self):
        self.fy.wait_recv()
        self.cd0.start()
        self.fx.wait_recv()
        self.cd1.start()

    def finish(self):
        self.local.wait()
        self.c.wait_recv(); self.cx.wait_recv(); self.cy.wait_recv()
        self.cd0.wait_recv(); self.cd1.wait_recv()

    def drain(self):
        for k in (self.x, self.y, self.c, self.fx, self.fy, self.cx, self.cy, self.cd0, self.cd1):
            k.wait_send()


def gather_kernel(nb, nw, *refs):
    x_ref, ws = refs[0], refs[1:1 + nw]
    xall, outs = refs[1 + nw], refs[2 + nw:2 + 2 * nw]
    zs, zr, ws_s, ws_r, ls = refs[2 + 2 * nw:]
    p = Place()
    enter(p, nb, True, "near")
    line = LineGather(p, nb, x_ref, xall, zs, zr)
    own = pltpu.make_async_copy(x_ref, xall.at[p.b], ls.at[nw])
    g = [PlaneGather(p, ws[i], outs[i], ws_s.at[i], ws_r.at[i], ls.at[i]) for i in range(nw)]
    n0 = nw - 2
    line.start(0)
    own.start()
    for k in g[:n0 + 1]:
        k.start()
    for k in g[:n0]:
        k.forward()
    g[n0 + 1].start()
    line.wait_recv(0)
    if nb > 2:
        line.start(1)
    g[n0].forward()
    for t in range(1, nb - 2):
        line.wait_recv(t)
        line.start(t + 1)
    g[n0 + 1].forward()
    for k in g:
        k.diag()
    line.wait_recv(nb - 2)
    for k in g:
        k.finish()
    own.wait()
    for t in range(nb - 1):
        line.wait_send(t)
    for k in g:
        k.drain()


def gather_all(x, weights, nb):
    nw = len(weights)
    outs = (jax.ShapeDtypeStruct((nb,) + x.shape, x.dtype),) + tuple(
        jax.ShapeDtypeStruct((8,) + w.shape, w.dtype) for w in weights
    )
    return pl.pallas_call(
        functools.partial(gather_kernel, nb, nw),
        out_shape=outs,
        in_specs=[VM] * (1 + nw),
        out_specs=(ANY,) * (1 + nw),
        scratch_shapes=[
            pltpu.SemaphoreType.DMA((2, nb - 1)),
            pltpu.SemaphoreType.DMA((2, nb - 1)),
            pltpu.SemaphoreType.DMA((nw, 9)),
            pltpu.SemaphoreType.DMA((nw, 9)),
            pltpu.SemaphoreType.DMA((nw + 1,)),
        ],
        compiler_params=pltpu.CompilerParams(
            collective_id=1, has_side_effects=True, vmem_limit_bytes=VMEM_LIMIT
        ),
        name="gather_all",
    )(x, *weights)


def line_kernel(nb, na, *refs):
    ins, outs = refs[:na], refs[na:2 * na]
    zs, zr, ls = refs[2 * na:]
    p = Place()
    enter(p, nb, False, "near")
    lines = [LineGather(p, nb, ins[i], outs[i], zs.at[i], zr.at[i]) for i in range(na)]
    own = [pltpu.make_async_copy(ins[i], outs[i].at[p.b], ls.at[i]) for i in range(na)]
    for k in lines:
        k.start(0)
    for k in own:
        k.start()
    for t in range(nb - 1):
        for k in lines:
            k.wait_recv(t)
            if t + 1 < nb - 1:
                k.start(t + 1)
    for k in own:
        k.wait()
    for t in range(nb - 1):
        for k in lines:
            k.wait_send(t)


def line_gather(arrays, nb):
    na = len(arrays)
    return pl.pallas_call(
        functools.partial(line_kernel, nb, na),
        out_shape=tuple(jax.ShapeDtypeStruct((nb,) + a.shape, a.dtype) for a in arrays),
        in_specs=[VM] * na,
        out_specs=(ANY,) * na,
        scratch_shapes=[
            pltpu.SemaphoreType.DMA((na, 2, nb - 1)),
            pltpu.SemaphoreType.DMA((na, 2, nb - 1)),
            pltpu.SemaphoreType.DMA((na,)),
        ],
        compiler_params=pltpu.CompilerParams(
            collective_id=2, has_side_effects=True, vmem_limit_bytes=VMEM_LIMIT
        ),
        name="line_gather",
    )(*arrays)


def row_loop(rows, chunk, body):
    if rows == chunk:
        body(0)
    else:
        def step(i, _):
            body(pl.multiple_of(i * chunk, chunk))
            return 0
        lax.fori_loop(0, rows // chunk, step, 0)


class PlaneReduce:
    def __init__(self, p, nb, g, out, buf, ss, rs):
        self.p, self.nb, self.g, self.out = p, nb, g, out
        self.A, self.P, self.BX, self.BY, self.CX, self.CY, self.F, self.Z, self.O = buf
        self.R, self.C = g.shape[-2:]
        self.dt = g.dtype
        self.ss, self.rs = ss, rs
        R, C = self.R, self.C
        h = R // 2
        self.h = h
        lo, hi = pl.ds(0, h), pl.ds(h, h)
        self.chunk = 16 if C > 1024 else (48 if h % 48 == 0 else h)
        self.cA = rcopy(g.at[:, :, 1 - p.c], self.A, ss.at[0], rs.at[0], p.C)
        self.cBX = rcopy(self.P.at[:, 1 - p.x, lo], self.BX, ss.at[1], rs.at[1], p.X)
        self.cBY = rcopy(self.P.at[1 - p.s, :, hi], self.BY, ss.at[2], rs.at[2], p.Y)
        self.cCX = rcopy(self.P.at[p.s, 1 - p.x, hi], self.CX, ss.at[3], rs.at[3], p.X)
        self.cCY = rcopy(self.P.at[1 - p.s, p.x, lo], self.CY, ss.at[4], rs.at[4], p.Y)

    def quarter(self, ref, j):
        R, C = self.R, self.C
        if isinstance(j, int):
            return ref.at[pl.ds((j // 2) * (R // 2), R // 2), pl.ds((j % 2) * (C // 2), C // 2)]
        r = pl.multiple_of((j // 2) * (R // 2), R // 2)
        c = pl.multiple_of((j % 2) * (C // 2), C // 2)
        return ref.at[pl.ds(r, R // 2), pl.ds(c, C // 2)]

    def a_start(self):
        self.cA.start()

    def b_start(self):
        self.cA.wait_recv()
        p, g, A, P, dt = self.p, self.g, self.A, self.P, self.dt

        def block(i, _):
            s, x = i // 2, i % 2

            def body(r):
                rows = pl.ds(r, self.chunk)
                P[s, x, rows] = (
                    g[s, x, p.c, rows].astype(jnp.float32) + A[s, x, rows].astype(jnp.float32)
                ).astype(dt)
            row_loop(self.R, self.chunk, body)
            return 0
        lax.fori_loop(0, 4, block, 0)
        self.cBX.start()
        self.cBY.start()

    def _add(self, dst, src):
        def body(r):
            rows = pl.ds(r, self.chunk)
            dst[rows] = (dst[rows].astype(jnp.float32) + src[rows].astype(jnp.float32)).astype(self.dt)
        row_loop(self.h, self.chunk, body)

    def c_start(self):
        p, h = self.p, self.h
        lo, hi = pl.ds(0, h), pl.ds(h, h)
        self.cBX.wait_recv()
        self._add(self.P.at[1 - p.s, p.x, lo], self.BX.at[1 - p.s])
        self.cCY.start()
        self.cBY.wait_recv()
        self._add(self.P.at[p.s, 1 - p.x, hi], self.BY.at[1 - p.x])
        self.cCX.start()
        self._add(self.P.at[p.s, p.x, lo], self.BX.at[p.s])
        self._add(self.P.at[p.s, p.x, hi], self.BY.at[p.x])

    def _z1(self, j, slot):
        return rcopy(self.quarter(self.F, j), self.Z.at[slot], self.ss.at[5 + j], self.rs.at[5 + slot], self.p.z(j))

    def _z2(self, j, slot):
        q = self.quarter(self.O, slot)
        return rcopy(q, q, self.ss.at[5 + self.nb + j], self.rs.at[5 + self.nb + slot], self.p.z(j))

    def d_start(self):
        p, h, nb = self.p, self.h, self.nb
        self.cCY.wait_recv()
        self.cCX.wait_recv()

        def lo_body(r):
            rows = pl.ds(r, self.chunk)
            self.F[rows] = (
                self.P[p.s, p.x, rows].astype(jnp.float32) + self.CY[rows].astype(jnp.float32)
            ).astype(self.dt)
        row_loop(h, self.chunk, lo_body)

        def hi_body(r):
            rows = pl.ds(r + h, self.chunk)
            self.F[rows] = (
                self.P[p.s, p.x, rows].astype(jnp.float32)
                + self.CX[pl.ds(r, self.chunk)].astype(jnp.float32)
            ).astype(self.dt)
        row_loop(h, self.chunk, hi_body)
        for j in range(nb):
            @pl.when(p.b != j)
            def _():
                self._z1(j, p.b).start()

    def e_start(self):
        p, nb = self.p, self.nb
        mine = self.quarter(self.F, p.b)
        total = self.quarter(self.O, p.b)
        for i in range(nb):
            @pl.when(p.b != i)
            def _():
                self._z1(i, i).wait_recv()

        def body(r):
            rows = pl.ds(r, self.chunk)
            acc = mine[rows].astype(jnp.float32)
            for d in range(1, nb):
                acc = acc + self.Z[(p.b + d) % nb, rows].astype(jnp.float32)
            total[rows] = acc.astype(self.dt)
        row_loop(self.h, self.chunk, body)
        for j in range(nb):
            @pl.when(p.b != j)
            def _():
                self._z2(j, p.b).start()

    def finish(self):
        p, nb = self.p, self.nb
        for i in range(nb):
            @pl.when(p.b != i)
            def _():
                self._z2(i, i).wait_recv()

        def body(r):
            rows = pl.ds(r, self.chunk)
            self.out[rows] = self.O[rows].astype(jnp.float32)
        row_loop(self.R, self.chunk, body)

    def drain(self):
        for k in (self.cA, self.cBX, self.cBY, self.cCX, self.cCY):
            k.wait_send()
        for j in range(self.nb):
            @pl.when(self.p.b != j)
            def _():
                self._z1(j, self.p.b).wait_send()
                self._z2(j, self.p.b).wait_send()


def reduce_scratch(shape, dt, nb):
    R, C = shape
    h = R // 2
    return [
        pltpu.VMEM((2, 2, R, C), dt),
        pltpu.VMEM((2, 2, R, C), dt),
        pltpu.VMEM((2, h, C), dt),
        pltpu.VMEM((2, h, C), dt),
        pltpu.VMEM((h, C), dt),
        pltpu.VMEM((h, C), dt),
        pltpu.VMEM((R, C), dt),
        pltpu.VMEM((nb, h, C // 2), dt),
        pltpu.VMEM((R, C), dt),
    ]


def wave(items, stages):
    n, m = len(items), len(stages)
    for step in range(n + m - 1):
        for k in range(m):
            i = step - k
            if 0 <= i < n:
                getattr(items[i], stages[k])()


def reduce_kernel(nb, nw, *refs):
    gs, outs = refs[:nw], refs[nw:2 * nw]
    bufs = refs[2 * nw:2 * nw + 9 * nw]
    ss, rs = refs[11 * nw:]
    p = Place()
    enter(p, nb, True, "all")
    items = [
        PlaneReduce(p, nb, gs[i], outs[i], bufs[9 * i:9 * i + 9], ss.at[i], rs.at[i]) for i in range(nw)
    ]
    for k in items:
        k.a_start()
    wave(items, ("b_start", "c_start", "d_start", "e_start"))
    for k in items:
        k.finish()
    for k in items:
        k.drain()


def reduce_all(grads, nb):
    nw = len(grads)
    scratch = []
    for g in grads:
        scratch += reduce_scratch(g.shape[-2:], g.dtype, nb)
    ns = 5 + 2 * nb
    return pl.pallas_call(
        functools.partial(reduce_kernel, nb, nw),
        out_shape=tuple(jax.ShapeDtypeStruct(g.shape[-2:], jnp.float32) for g in grads),
        in_specs=[VM] * nw,
        out_specs=(VM,) * nw,
        scratch_shapes=scratch + [pltpu.SemaphoreType.DMA((nw, ns)), pltpu.SemaphoreType.DMA((nw, ns))],
        compiler_params=pltpu.CompilerParams(
            collective_id=3, has_side_effects=True, vmem_limit_bytes=VMEM_LIMIT
        ),
        name="reduce_all",
    )(*grads)


HEAD_DIM = 64
PAIR = 128
MASKED = -1e30
TILE = 256


def dot(a, b, ca, cb):
    return lax.dot_general(a, b, (((ca,), (cb,)), ((), ())), preferred_element_type=jnp.float32)


def left_lanes(shape):
    return lax.broadcasted_iota(jnp.int32, shape, 1) < HEAD_DIM


def one_head(pair, left, first):
    keep = left if first else jnp.logical_not(left)
    return jnp.where(keep, pair, jnp.zeros_like(pair))


def attn_fwd_kernel(span, col_ref, row_ref, q_ref, k_ref, v_ref, o_ref, ob_ref, lse_ref, m_ref, l_ref, acc_ref):
    rows = q_ref.shape[0]
    left = left_lanes((rows, PAIR))
    m_ref[...] = jnp.full_like(m_ref, MASKED)
    l_ref[...] = jnp.zeros_like(l_ref)
    acc_ref[...] = jnp.zeros_like(acc_ref)
    q = q_ref[...]
    heads = [one_head(q, left, True), one_head(q, left, False)]
    codes = col_ref[...]

    def step(t, _):
        at = pl.multiple_of(t * TILE, TILE)
        k = k_ref[pl.ds(at, TILE), :]
        v = v_ref[pl.ds(at, TILE), :]
        mask = codes == row_ref[:, pl.ds(at, TILE)]
        alphas, parts = [], []
        for i in range(2):
            s = jnp.where(mask, dot(heads[i], k, 1, 1), MASKED)
            old = m_ref[i]
            new = jnp.maximum(old, jnp.max(s, axis=1, keepdims=True))
            p = jnp.exp(s - new)
            alpha = jnp.exp(old - new)
            m_ref[i] = new
            l_ref[i] = l_ref[i] * alpha + jnp.sum(p, axis=1, keepdims=True)
            alphas.append(alpha)
            parts.append(dot(p.astype(jnp.bfloat16), v, 1, 0))
        acc_ref[...] = acc_ref[...] * jnp.where(left, alphas[0], alphas[1]) + jnp.where(left, parts[0], parts[1])
        return 0

    lax.fori_loop(span[0], span[1], step, 0)
    total = jnp.where(left, l_ref[0], l_ref[1])
    o = acc_ref[...] / total
    o_ref[...] = o
    ob_ref[...] = o.astype(jnp.bfloat16)
    lse_ref[...] = jnp.where(left, m_ref[0], m_ref[1]) + jnp.log(total)


def attention(q, k_all, v_all, codes, own_codes, span):
    rows, width = q.shape
    total = k_all.shape[0]
    pairs = width // PAIR
    own = pl.BlockSpec((rows, PAIR), lambda h, s: (0, h))
    every = pl.BlockSpec((total, PAIR), lambda h, s: (0, h))
    return pl.pallas_call(
        attn_fwd_kernel,
        grid_spec=pltpu.PrefetchScalarGridSpec(
            num_scalar_prefetch=1,
            grid=(pairs,),
            in_specs=[
                pl.BlockSpec((rows, 1), lambda h, s: (0, 0)),
                pl.BlockSpec((1, total), lambda h, s: (0, 0)),
                own, every, every,
            ],
            out_specs=[own, own, own],
            scratch_shapes=[
                pltpu.VMEM((2, rows, 1), jnp.float32),
                pltpu.VMEM((2, rows, 1), jnp.float32),
                pltpu.VMEM((rows, PAIR), jnp.float32),
            ],
        ),
        out_shape=[
            jax.ShapeDtypeStruct((rows, width), jnp.float32),
            jax.ShapeDtypeStruct((rows, width), jnp.bfloat16),
            jax.ShapeDtypeStruct((rows, width), jnp.float32),
        ],
        compiler_params=pltpu.CompilerParams(vmem_limit_bytes=48 << 20),
        name="attention",
    )(span, own_codes.reshape(rows, 1), codes.reshape(1, total), q, k_all, v_all)


def stats_kernel(g_ref, o_ref, lse_ref, out_ref, delta_ref):
    rows = g_ref.shape[0]
    left = left_lanes((rows, PAIR))
    t = g_ref[...].astype(jnp.float32) * o_ref[...]
    d0 = jnp.sum(jnp.where(left, t, 0.0), axis=1, keepdims=True)
    d1 = jnp.sum(jnp.where(left, 0.0, t), axis=1, keepdims=True)
    delta_ref[...] = jnp.where(left, d0, d1)
    lane = lax.broadcasted_iota(jnp.int32, (rows, PAIR), 1)
    lse = lse_ref[...]
    packed = jnp.where(lane == 0, lse[:, :1], jnp.where(lane == 1, lse[:, HEAD_DIM:HEAD_DIM + 1], jnp.where(lane == 2, d0, d1)))
    out_ref[0] = packed.T[:8]


def row_stats(grad, o, lse):
    rows, width = grad.shape
    pairs = width // PAIR
    own = pl.BlockSpec((rows, PAIR), lambda h: (0, h))
    return pl.pallas_call(
        stats_kernel,
        grid=(pairs,),
        in_specs=[own, own, own],
        out_specs=[pl.BlockSpec((1, 8, rows), lambda h: (h, 0, 0)), own],
        out_shape=[
            jax.ShapeDtypeStruct((pairs, 8, rows), jnp.float32),
            jax.ShapeDtypeStruct((rows, width), jnp.float32),
        ],
        name="row_stats",
    )(grad, o, lse)


def attn_bwd_kernel(span, col_ref, row_ref, q_ref, k_ref, v_ref, g_ref, lse_ref, delta_ref,
                    qa_ref, ka_ref, va_ref, ga_ref, st_ref, r_ref, rk_ref, rv_ref, dq_ref, dk_ref, dv_ref):
    rows = q_ref.shape[0]
    left = left_lanes((rows, PAIR))
    dq_ref[...] = jnp.zeros_like(dq_ref)
    dk_ref[...] = jnp.zeros_like(dk_ref)
    dv_ref[...] = jnp.zeros_like(dv_ref)
    codes = col_ref[...]
    qs = [one_head(q_ref[...], left, i == 0) for i in range(2)]
    ks = [one_head(k_ref[...], left, i == 0) for i in range(2)]
    vs = [one_head(v_ref[...], left, i == 0) for i in range(2)]
    gs = [one_head(g_ref[...], left, i == 0) for i in range(2)]
    lses = [lse_ref[:, i * HEAD_DIM:i * HEAD_DIM + 1] for i in range(2)]
    deltas = [delta_ref[:, i * HEAD_DIM:i * HEAD_DIM + 1] for i in range(2)]

    def step(t, _):
        at = pl.multiple_of(t * TILE, TILE)
        tile = pl.ds(at, TILE)
        mask = codes == row_ref[:, tile]
        k, v, q, g = ka_ref[tile, :], va_ref[tile, :], qa_ref[tile, :], ga_ref[tile, :]
        dqs, dks, dvs = [], [], []
        for i in range(2):
            s = jnp.where(mask, dot(qs[i], k, 1, 1), MASKED)
            p = jnp.exp(s - lses[i])
            dp = dot(gs[i], v, 1, 1)
            ds = (p * (dp - deltas[i])).astype(jnp.bfloat16)
            dqs.append(dot(ds, k, 1, 0))
            st = jnp.where(mask, dot(ks[i], q, 1, 1), MASKED)
            pt = jnp.exp(st - st_ref[0, i:i + 1, tile])
            dvs.append(dot(pt.astype(jnp.bfloat16), g, 1, 0))
            dpt = dot(vs[i], g, 1, 1)
            dst = (pt * (dpt - st_ref[0, 2 + i:3 + i, tile])).astype(jnp.bfloat16)
            dks.append(dot(dst, q, 1, 0))
        dq_ref[...] += jnp.where(left, dqs[0], dqs[1])
        dk_ref[...] += jnp.where(left, dks[0], dks[1])
        dv_ref[...] += jnp.where(left, dvs[0], dvs[1])
        return 0

    lax.fori_loop(span[0], span[1], step, 0)
    r_ref[...] = dq_ref[...] * (HEAD_DIM ** (-0.5))
    rk_ref[...] = dk_ref[...].astype(jnp.bfloat16)
    rv_ref[...] = dv_ref[...]


def attention_grad(q, k, v, g, lse, delta, q_all, k_all, v_all, g_all, stats, codes, own_codes, span):
    rows, width = q.shape
    total = k_all.shape[0]
    pairs = width // PAIR
    own = pl.BlockSpec((rows, PAIR), lambda h, s: (0, h))
    every = pl.BlockSpec((total, PAIR), lambda h, s: (0, h))
    return pl.pallas_call(
        attn_bwd_kernel,
        grid_spec=pltpu.PrefetchScalarGridSpec(
            num_scalar_prefetch=1,
            grid=(pairs,),
            in_specs=[
                pl.BlockSpec((rows, 1), lambda h, s: (0, 0)),
                pl.BlockSpec((1, total), lambda h, s: (0, 0)),
                own, own, own, own, own, own, every, every, every, every,
                pl.BlockSpec((1, 8, total), lambda h, s: (h, 0, 0)),
            ],
            out_specs=[own, own, own],
            scratch_shapes=[pltpu.VMEM((rows, PAIR), jnp.float32)] * 3,
        ),
        out_shape=[
            jax.ShapeDtypeStruct((rows, width), jnp.float32),
            jax.ShapeDtypeStruct((rows, width), jnp.bfloat16),
            jax.ShapeDtypeStruct((rows, width), jnp.float32),
        ],
        compiler_params=pltpu.CompilerParams(vmem_limit_bytes=48 << 20),
        name="attention_grad",
    )(span, own_codes.reshape(rows, 1), codes.reshape(1, total), q, k, v, g, lse, delta, q_all, k_all, v_all, g_all, stats)


EPSILON = 1e-06
PLANE = ("seq", "shard")


def normalize(hidden, gain, shift):
    center = hidden - jnp.mean(hidden, axis=-1, keepdims=True)
    spread = jnp.mean(center * center, axis=-1, keepdims=True)
    return center * lax.rsqrt(spread + EPSILON) * gain + shift


def smooth_gate(hidden):
    return jax.nn.gelu(hidden, approximate=False)


def mm(left, right):
    return jnp.dot(left, right, preferred_element_type=jnp.float32)


def contract_rows(left, right):
    return dot(left, right, 0, 0)


def times_transpose(left, right):
    return dot(left, right, 1, 1)


def tuned_plane():
    return lax.axis_size("seq") == 2 and lax.axis_size("shard") == 4 and lax.axis_size("blk") == 4


def gather_inputs(x, mats, vecs):
    nb = lax.axis_size("blk")
    if not tuned_plane():
        x_all = lax.all_gather(x, "blk", axis=0)
        mats = [lax.all_gather(w, PLANE, axis=0, tiled=True) for w in mats]
        vecs = [lax.all_gather(v, PLANE, axis=0, tiled=True) for v in vecs]
        return x_all, mats, vecs
    sizes = [v.shape[0] for v in vecs]
    packed = jnp.concatenate(vecs)
    packed = jnp.pad(packed, (0, 32 * 128 - packed.shape[0])).reshape(32, 128)
    out = gather_all(x, [packed] + list(mats), nb)
    flat = out[1].reshape(8, 32 * 128)
    whole, at = [], 0
    for size in sizes:
        whole.append(flat[:, at:at + size].reshape(8 * size))
        at += size
    return out[0], [w.reshape(-1, w.shape[-1]) for w in out[2:]], whole


def gather_line(arrays):
    nb = lax.axis_size("blk")
    if not tuned_plane():
        return [lax.all_gather(a, "blk", axis=0) for a in arrays]
    return line_gather(arrays, nb)


def reduce_grads(mats, vecs):
    nb = lax.axis_size("blk")
    if not tuned_plane():
        def total(g):
            part = lax.psum_scatter(g.astype(jnp.bfloat16), PLANE, scatter_dimension=0, tiled=True)
            return lax.psum(part, "blk").astype(jnp.float32)
        return [total(g) for g in mats], [total(g) for g in vecs]
    rows = [v.shape[0] // 8 for v in vecs]
    packed = jnp.concatenate([v.reshape(8, -1) for v in vecs], axis=1)
    packed = jnp.pad(packed, ((0, 0), (0, 16 * 256 - packed.shape[1])))
    args = [g.astype(jnp.bfloat16).reshape(2, 2, 2, g.shape[0] // 8, g.shape[1]) for g in mats]
    out = reduce_all(args + [packed.reshape(2, 2, 2, 16, 256)], nb)
    flat = out[-1].reshape(-1)
    parts, at = [], 0
    for n in rows:
        parts.append(flat[at:at + n])
        at += n
    return list(out[:-1]), parts


def per_device(
    tokens, segments, live_mask, query_weight, key_weight, value_weight, out_weight,
    query_bias, value_bias, out_bias, first_gain, first_shift, up_weight, up_bias,
    down_weight, down_bias, second_gain, second_shift, cotangent,
):
    inputs = tokens[0]
    rows, width = inputs.shape
    nb = lax.axis_size("blk")
    place = lax.axis_index("blk")
    seg, live = segments[0], live_mask[0]
    total = seg.shape[0]
    x_all, mats, vecs = gather_inputs(
        inputs,
        [query_weight, key_weight, value_weight, out_weight, up_weight, down_weight],
        [query_bias, value_bias, out_bias, first_gain, first_shift, up_bias, down_bias, second_gain, second_shift],
    )
    wq, wk, wv, wo, wup, wdn = mats
    bq, bv, bo, g1, s1, bup, bdn, g2, s2 = [v.astype(jnp.float32) for v in vecs]
    start = place * rows
    codes = jnp.where(live > 0, seg, -1 - jnp.arange(total, dtype=jnp.int32))
    own_codes = lax.dynamic_slice_in_dim(codes, start, rows)
    own_seg = lax.dynamic_slice_in_dim(seg, start, rows)
    low = jnp.sum((seg < own_seg[0]).astype(jnp.int32))
    high = jnp.sum((seg <= own_seg[rows - 1]).astype(jnp.int32))
    span = jnp.stack([low // TILE, (high + TILE - 1) // TILE])

    xs = x_all.reshape(total, width)
    scale = HEAD_DIM ** (-0.5)
    q_all = ((mm(xs, wq) + bq) * scale).astype(jnp.bfloat16)
    k_all = mm(xs, wk).astype(jnp.bfloat16)
    v_all = (mm(xs, wv) + bv).astype(jnp.bfloat16)
    q, k, v = [lax.dynamic_slice_in_dim(a, start, rows) for a in (q_all, k_all, v_all)]
    summed, attended, lse = attention(q, k_all, v_all, codes, own_codes, span)

    first_sum = inputs.astype(jnp.float32) + (mm(attended, wo) + bo)
    first_norm, first_pull = jax.vjp(normalize, first_sum, g1, s1)
    first_low = first_norm.astype(jnp.bfloat16)
    hidden = mm(first_low, wup) + bup
    gated, gate_pull = jax.vjp(smooth_gate, hidden)
    gated_low = gated.astype(jnp.bfloat16)
    second_sum = first_norm + (mm(gated_low, wdn) + bdn)
    result, second_pull = jax.vjp(normalize, second_sum, g2, s2)
    second_grad, g2_grad, s2_grad = second_pull(cotangent[0].astype(jnp.float32))
    bdn_grad = jnp.sum(second_grad, axis=0)
    second_low = second_grad.astype(jnp.bfloat16)
    wdn_grad = contract_rows(gated_low, second_low)
    (hidden_grad,) = gate_pull(times_transpose(second_low, wdn))
    bup_grad = jnp.sum(hidden_grad, axis=0)
    hidden_low = hidden_grad.astype(jnp.bfloat16)
    wup_grad = contract_rows(first_low, hidden_low)
    norm_grad = second_grad + times_transpose(hidden_low, wup)
    first_grad, g1_grad, s1_grad = first_pull(norm_grad)
    bo_grad = jnp.sum(first_grad, axis=0)
    first_grad_low = first_grad.astype(jnp.bfloat16)
    wo_grad = contract_rows(attended, first_grad_low)
    do = times_transpose(first_grad_low, wo).astype(jnp.bfloat16)

    stats, delta = row_stats(do, summed, lse)
    do_all, stats_all = gather_line([do, stats])
    stats_all = jnp.transpose(stats_all, (1, 2, 0, 3)).reshape(stats.shape[0], 8, total)
    r, rk, dv = attention_grad(
        q, k, v, do, lse, delta, q_all, k_all, v_all, do_all.reshape(total, width), stats_all,
        codes, own_codes, span,
    )
    bq_grad = jnp.sum(r, axis=0)
    bv_grad = jnp.sum(dv, axis=0)
    rq = r.astype(jnp.bfloat16)
    rv = dv.astype(jnp.bfloat16)
    wq_grad = contract_rows(inputs, rq)
    wk_grad = contract_rows(inputs, rk)
    wv_grad = contract_rows(inputs, rv)
    token_grad = first_grad + times_transpose(rq, wq) + times_transpose(rk, wk) + times_transpose(rv, wv)

    big, small = reduce_grads(
        [wdn_grad, wup_grad, wo_grad, wq_grad, wk_grad, wv_grad],
        [bq_grad, bv_grad, bo_grad, g1_grad, s1_grad, bup_grad, bdn_grad, g2_grad, s2_grad],
    )
    rdn, rup, ro, rwq, rwk, rwv = big
    return (
        result.astype(jnp.bfloat16)[None], token_grad.astype(jnp.bfloat16)[None],
        rwq, rwk, rwv, ro, small[0], small[1], small[2], small[3], small[4],
        rup, small[5], rdn, small[6], small[7], small[8],
    )


def solution(mesh):
    flat = P(PLANE, "blk", None)
    mat = P(PLANE, None)
    vec = P(PLANE)
    return jax.shard_map(
        per_device,
        mesh=mesh,
        in_specs=(
            flat, mat, mat, mat, mat, mat, mat, vec, vec, vec, vec, vec, mat, vec, mat, vec, vec, vec, flat,
        ),
        out_specs=(flat, flat, mat, mat, mat, mat, vec, vec, vec, vec, vec, mat, vec, mat, vec, vec, vec),
        check_vma=False,
    )
```

time: 994 us -> 600 us (0.60)
  the two profiles are of different devices: /device:TPU:0 before, /device:TPU:1 now
where the time goes in v1:
time: 600 us; the launch traced here: 590 us
  Pallas kernels  454 us (76%)
  matrix products  89.9 us (15%)
  local copies, waits for them, and re-layouts  30.3 us (5%)
  other arithmetic  11.1 us (2%)
    pallas_call x1, Pallas kernels, reduce_all(): pl.pallas_call(functools.partial(reduce_kernel, nb, nw), out_shape=tuple(...  179 us
    pallas_call x1, Pallas kernels, line_gather(): pl.pallas_call(functools.partial(line_kernel, nb, na), out_shape=tuple((j...  120 us
    pallas_call x1, Pallas kernels, gather_all(): pl.pallas_call(functools.partial(gather_kernel, nb, nw), out_shape=outs,...  67.2 us
    pallas_call x1, Pallas kernels, attention(): pl.pallas_call(attn_fwd_kernel, grid_spec=pltpu.PrefetchScalarGridSpec(nu...  53.4 us
    dot_general x6, matrix products, mm(): return jnp.dot(left, right, preferred_element_type=jnp.float32)  45.4 us
    dot_general x12, matrix products, dot(): lax.dot_general(a, b, (((ca,), (cb,)), ((), ())), preferred_element_type=...  44.5 us
    pallas_call x1, Pallas kernels, attention_grad(): pl.pallas_call(attn_bwd_kernel, grid_spec=pltpu.PrefetchScalarGridSpec(nu...  28.2 us
    unnamed x77, local copies, waits for them, and re-layouts  17 us

profile of v1, /device:TPU:1, one launch (start us, length us, event | category | flops | bytes accessed | tf_op | source)
XLA Modules:
  0.0 590.0 jit_solution(9143992916483933823)
XLA Ops:
  0.7 1.3 constant_dynamic-slice_fusion.4
  1.9 2.6 convert_reduce_fusion.2
  7.9 6.1 %concatenate.6 = bf16[1152]{0:T(1024)(128)(2,1)S(1)} concatenate(bf16[96]{0:T(256)(128)(2,1)} %param.26, bf16[96]{0:T(256)(128)(2,1)} %param.27, bf16[96]{0:T(256)(128)(2,1)} %param.28, bf16[96]{0:T(256)(128)(2,1)} %param.29, bf16[96]{0:T(256)(128)(2,1)} %param.30, bf16[384]{0:T(512)(128)(2,1)} %param.32, bf16[96]{0:T(256)(128)(2,1)} %param.34, bf16[96]{0:T(256)(128)(2,1)} %param.35, ...), dimensions={0} | concatenate | bytes 4608 | tf_op jit(solution)/shard_map/concatenate | solution.py:689
  14.0 0.6 pad_bitcast_fusion.refs_1_
  14.6 67.2 %gather_all.1 = (bf16[4,512,768]{2,1,0:T(8,128)(2,1)}, bf16[8,32,128]{2,1,0:T(8,128)(2,1)}, bf16[8,96,768]{2,1,0:T(8,128)(2,1)}, bf16[8,96,768]{2,1,0:T(8,128)(2...) custom-call(bf16[512,768]{1,0:T(8,128)(2,1)} %bitcast.92, ...), custom_call_target="tpu_custom_call" | custom-call | tf_op jit(solution)/shard_map/gather_all/pallas_call | solution.py:186
  81.9 0.9 copy.44
  82.9 4.8 multiply_convert_fusion.1.qa_ref
  87.7 1.7 copy-done.17
  89.6 1.1 copy-done.18
  90.8 6.4 %add_convert_fusion.v_ref.va_ref = bf16[2048,768]{1,0:T(8,128)(2,1)} fusion(bf16[2048,768]{1,0:T(8,128)(2,1)} %bitcast.121, bf16[768,768]{1,0:T(8,128)(2,1)S(1)} %bitcast.98, f32[768]{0:T(1024)S(1)} %reshape.305), kind=kOutput, calls=%fused_computation.16 | convolution fusion | flops 2419064832 | bytes 7474176 | tf_op jit(solution)/shard_map/dot_general | solution.py:666
  97.2 4.5 convolution_convert_fusion.2.k_ref.ka_ref
  101.7 0.1 dynamic-slice_select_fusion
  101.8 0.1 copy.37.col_ref
  102.0 53.4 %attention.1 = (f32[512,768]{1,0:T(8,128)S(1)}, bf16[512,768]{1,0:T(8,128)(2,1)S(1)}, f32[512,768]{1,0:T(8,128)S(1)}) custom-call(s32[2]{0:T(128)S(1)} %pad_add_fusion.span, s32[512,1]{1,0:T(8,128)S(1)} %copy.37.col_ref, s32[1,2048]{1,0:T(1,128)S(1)} %compare_select_fusion.row_ref, bf16[512,768]{1,0:T(8,128)(2,1)S(1)} %constant_dynamic-slice_fusion.3.q_ref, ...), custom_call_target="tpu_custom_call" | custom-call | tf_op jit(solution)/shard_map/attention/pallas_call | solution.py:520
  155.4 1.1 copy-done.1
  156.5 1.2 copy-done.2
  157.8 2.2 fusion.39
  159.9 1.1 copy-done.11
  161.1 0.3 multiply_reduce_fusion.3
  161.6 21.0 %multiply_convert_fusion = (bf16[512,3072]{1,0:T(8,128)(2,1)}, f32[512,3072]{1,0:T(8,128)}, f32[512,3072]{1,0:T(8,128)}) fusion(f32[3072]{0:T(1024)S(1)} %reshape.309, bf16[768,3072]{1,0:T(8,128)(2,1)} %bitcast.116, f32[512,768]{1,0:T(8,128)} %copy-done.11, f32[768]{0:T(1024)S(1)} %reshape.308, f32[768]{0:T(1024)S(1)} %reshape.307, f32[512]{0:T(512)S(1)} %fusion.26, ...), kind=kOutput, calls=%fused_computation.3 | convolution fusion | flops 2521694208 | bytes 22042624 | tf_op jit(solution)/shard_map/dot_general | solution.py:666
  182.7 6.5 %fusion.40 = (f32[512]{0:T(512)S(1)}, f32[512,768]{1,0:T(8,128)S(1)}) fusion(f32[768]{0:T(1024)S(1)} %reshape.310, bf16[512,3072]{1,0:T(8,128)(2,1)} %get-tuple-element.78, bf16[3072,768]{1,0:T(8,128)(2,1)} %bitcast.118, f32[768]{0:T(1024)S(1)} %reshape.308, f32[768]{0:T(1024)S(1)} %reshape.307, f32[512]{0:T(512)S(1)} %fusion.26, ...), kind=kOutput, calls=%fused_computation.104 | convolution fusion | flops 2418671104 | bytes 11025408 | tf_op jit(solution)/shard_map/dot_general | solution.py:666
  189.2 0.3 multiply_reduce_fusion.2
  189.5 1.9 fusion.11
  191.5 2.7 fusion.36
  194.3 1.2 copy-done.14
  195.4 0.2 add_reduce_fusion.1
  195.7 11.0 %fusion.41 = (f32[3072]{0:T(1024)S(1)}, bf16[512,3072]{1,0:T(8,128)(2,1)S(1)}) fusion(f32[512,3072]{1,0:T(8,128)} %get-tuple-element.79, bf16[3072,768]{1,0:T(8,128)(2,1)} %bitcast.119, f32[512,768]{1,0:T(8,128)} %copy-done.14, f32[512]{0:T(512)S(1)} %negate_multiply_fusion.2, f32[512,3072]{1,0:T(8,128)} %get-tuple-element.101, f32[3072]{0:T(1024)S(1)} %reshape.309), kind=kOutput, calls=%fused_computation.105 | convolution fusion | flops 2441868288 | bytes 22046720 | tf_op jit(solution)/shard_map/dot_general | solution.py:465
  206.8 6.6 %multiply_reduce_fusion = (f32[768]{0:T(1024)S(1)}, f32[512]{0:T(512)S(1)}, f32[768]{0:T(1024)S(1)}, f32[512,768]{1,0:T(8,128)S(1)}) fusion(f32[512,768]{1,0:T(8,128)S(1)} %copy-done.12, f32[512]{0:T(512)S(1)} %fusion.26, f32[512]{0:T(512)S(1)} %broadcast_multiply_fusion.1, f32[768]{0:T(1024)S(1)} %reshape.307, bf16[768,3072]{1,0:T(8,128)(2,1)} %bitcast.117, ...), kind=kOutput, calls=%fused_computation.32 | convolution fusion | flops 2419849216 | bytes 12600320 | tf_op jit(solution)/shard_map/dot_general | solution.py:465
  213.4 0.6 fusion.35
  214.0 0.2 add_reduce_fusion
  214.3 3.3 convolution_convert_fusion.7.g_ref.refs_0_
  217.6 6.1 %row_stats.1 = (f32[6,8,512]{2,1,0:T(8,128)}, f32[512,768]{1,0:T(8,128)}) custom-call(bf16[512,768]{1,0:T(8,128)(2,1)} %convolution_convert_fusion.7.g_ref.refs_0_, f32[512,768]{1,0:T(8,128)} %copy-done.2, f32[512,768]{1,0:T(8,128)} %copy-done.1), custom_call_target="tpu_custom_call" | custom-call | tf_op jit(solution)/shard_map/row_stats/pallas_call | solution.py:564
  223.7 120.0 %line_gather.1 = (bf16[4,512,768]{2,1,0:T(8,128)(2,1)}, f32[4,6,8,512]{3,2,1,0:T(8,128)}) custom-call(bf16[512,768]{1,0:T(8,128)(2,1)} %convolution_convert_fusion.7.g_ref.refs_0_, f32[6,8,512]{2,1,0:T(8,128)} %get-tuple-element.54.refs_1_), custom_call_target="tpu_custom_call" | custom-call | tf_op jit(solution)/shard_map/line_gather/pallas_call | solution.py:230
  343.7 1.0 copy.38
  344.7 1.6 constant_dynamic-slice_fusion.1
  346.3 28.2 %attention_grad.1 = (f32[512,768]{1,0:T(8,128)S(1)}, bf16[512,768]{1,0:T(8,128)(2,1)S(1)}, f32[512,768]{1,0:T(8,128)}) custom-call(s32[2]{0:T(128)S(1)} %pad_add_fusion.span, s32[512,1]{1,0:T(8,128)S(1)} %copy.37.col_ref, s32[1,2048]{1,0:T(1,128)S(1)} %compare_select_fusion.row_ref, bf16[512,768]{1,0:T(8,128)(2,1)S(1)} %constant_dynamic-slice_fusion.3.q_ref, ...), custom_call_target="tpu_custom_call" | custom-call | tf_op jit(solution)/shard_map/attention_grad/pallas_call | solution.py:627
  374.6 0.9 copy-done.3
  375.4 0.1 reduce_sum.183
  375.6 1.6 reduce_sum.184
  377.5 0.2 convert_reduce_fusion
  377.7 0.1 concatenate.7
  377.9 0.7 copy.41
  378.6 3.4 convolution_convert_fusion.6
  382.0 6.6 %convolution_convert_fusion = bf16[768,3072]{1,0:T(8,128)(2,1)} fusion(bf16[512,3072]{1,0:T(8,128)(2,1)} %copy-done.32, f32[512,768]{1,0:T(8,128)S(1)} %copy-done.13, f32[768]{0:T(1024)S(1)} %reshape.308, f32[768]{0:T(1024)S(1)} %reshape.307, f32[512]{0:T(512)S(1)} %fusion.26, f32[512]{0:T(512)S(1)} %broadcast_multiply_fusion.1), kind=kOutput, calls=%fused_computation.19 | convolution fusion | flops 2420244480 | bytes 9447424 | tf_op jit(solution)/shard_map/dot_general | solution.py:465
  388.6 4.5 convolution_convert_fusion.1
  393.1 1.9 convolution_convert_fusion.5
  395.0 1.9 convolution_convert_fusion.4
  396.9 1.9 convolution_convert_fusion.3
  398.7 179.3 %reduce_all.1 = (f32[384,768]{1,0:T(8,128)}, f32[96,3072]{1,0:T(8,128)}, f32[96,768]{1,0:T(8,128)}, f32[96,768]{1,0:T(8,128)}, f32[96,768]{1,0:T(8,128)}, /*index=5*/f32[96,768]{1,0:T(8,128)}, f32[16,256]{1,0:T(8,128)}) custom-call(bf16[2,2,2,384,768]{4,3,2,1,0:T(8,128)(2,1)} %bitcast.96, bf16[2,2,2,96,3072]{4,3,2,1,0:T(8,128)(2,1)} %bitcast.95, ...), custom_call_target="tpu_custom_call" | custom-call | tf_op jit(solution)/shard_map/reduce_all/pallas_call | solution.py:445
  578.0 0.7 copy.42
  578.8 0.6 fusion.38
  579.4 0.6 slice.96
  580.0 0.8 fusion.24
  580.8 0.4 copy-done.31
  581.3 0.8 fusion.42
  582.1 0.6 copy-done.7
  582.7 0.3 copy-done.19
  583.0 1.8 fusion.18
  584.8 0.7 copy.51
  585.5 0.7 copy.52
  586.3 0.7 copy.53
  587.0 0.7 copy.54
  587.7 1.0 copy.55
  588.7 1.0 copy.56
  (91 shorter events, 1.7 us)
Async XLA Ops:
  87.7 1.8 copy-start.17
  89.5 1.3 copy-start.18
  90.8 6.4 %copy-start.29 = (bf16[4,512,768]{2,1,0:T(8,128)(2,1)S(1)}, bf16[4,512,768]{2,1,0:T(8,128)(2,1)}, u32[]{:S(2)}) copy-start(bf16[4,512,768]{2,1,0:T(8,128)(2,1)} %get-tuple-element.42) | copy-start | bytes 9437188
  90.8 6.4 %copy-start.30 = (bf16[8,96,768]{2,1,0:T(8,128)(2,1)S(1)}, bf16[8,96,768]{2,1,0:T(8,128)(2,1)}, u32[]{:S(2)}) copy-start(bf16[8,96,768]{2,1,0:T(8,128)(2,1)} %get-tuple-element.45) | copy-start | bytes 3538948
  97.2 4.5 copy-start.28
  97.2 4.5 copy-start.27
  102.0 55.8 %copy-start.9 = (bf16[1,512,768]{2,1,0:T(8,128)(2,1)S(1)}, bf16[1,512,768]{2,1,0:T(8,128)(2,1)}, u32[]{:S(2)}) copy-start(bf16[1,512,768]{2,1,0:T(8,128)(2,1)} %param.19) | copy-start | bytes 2359300
  155.4 1.1 copy-start.1
  156.5 1.2 copy-start.2
  159.9 1.1 copy-start.11
  194.3 1.2 copy-start.14
  195.7 11.0 %copy-start.12 = (f32[512,768]{1,0:T(8,128)S(1)}, f32[512,768]{1,0:T(8,128)}, u32[]{:S(2)}) copy-start(f32[512,768]{1,0:T(8,128)} %copy-done.11) | copy-start | bytes 4718596
  195.7 11.0 %copy-start.15 = (f32[512,768]{1,0:T(8,128)S(1)}, f32[512,768]{1,0:T(8,128)}, u32[]{:S(2)}) copy-start(f32[512,768]{1,0:T(8,128)} %copy-done.14) | copy-start | bytes 4718596
  206.7 6.6 %copy-start.32 = (bf16[512,3072]{1,0:T(8,128)(2,1)}, bf16[512,3072]{1,0:T(8,128)(2,1)S(1)}, u32[]{:S(2)}) copy-start(bf16[512,3072]{1,0:T(8,128)(2,1)S(1)} %get-tuple-element.106) | copy-start | bytes 9437188
  214.0 3.6 copy-start.6
  344.7 1.6 copy-start
  374.6 0.9 copy-start.3
  375.4 2.1 copy-start.8
  378.6 3.4 copy-start.13
  382.0 6.6 %copy-start.16 = (f32[512,768]{1,0:T(8,128)S(1)}, f32[512,768]{1,0:T(8,128)}, u32[]{:S(2)}) copy-start(f32[512,768]{1,0:T(8,128)} %copy-done.14) | copy-start | bytes 4718596
  382.0 6.6 %copy-start.33 = (bf16[512,3072]{1,0:T(8,128)(2,1)S(1)}, bf16[512,3072]{1,0:T(8,128)(2,1)}, u32[]{:S(2)}) copy-start(bf16[512,3072]{1,0:T(8,128)(2,1)} %get-tuple-element.78) | copy-start | bytes 9437188
  388.6 4.5 copy-start.10
  393.1 1.9 copy-start.4
  395.0 1.9 copy-start.5
  398.7 181.3 %copy-start.22 = (bf16[8,96,768]{2,1,0:T(8,128)(2,1)S(1)}, bf16[8,96,768]{2,1,0:T(8,128)(2,1)}, u32[]{:S(2)}) copy-start(bf16[8,96,768]{2,1,0:T(8,128)(2,1)} %get-tuple-element.43) | copy-start | bytes 3538948
  580.0 1.3 copy-start.31
  581.3 1.4 copy-start.7
  581.3 1.7 copy-start.19
  583.0 1.8 copy-start.26
  583.0 2.5 copy-start.25
  583.0 3.2 copy-start.24
  584.8 2.2 copy-start.23
  584.8 2.9 copy-start.21
  587.0 1.7 copy-start.20

commit v2 on v1

--- a/solution.py
+++ b/solution.py
@@ -202,48 +202,6 @@
     )(x, *weights)
 
 
-def line_kernel(nb, na, *refs):
-    ins, outs = refs[:na], refs[na:2 * na]
-    zs, zr, ls = refs[2 * na:]
-    p = Place()
-    enter(p, nb, False, "near")
-    lines = [LineGather(p, nb, ins[i], outs[i], zs.at[i], zr.at[i]) for i in range(na)]
-    own = [pltpu.make_async_copy(ins[i], outs[i].at[p.b], ls.at[i]) for i in range(na)]
-    for k in lines:
-        k.start(0)
-    for k in own:
-        k.start()
-    for t in range(nb - 1):
-        for k in lines:
-            k.wait_recv(t)
-            if t + 1 < nb - 1:
-                k.start(t + 1)
-    for k in own:
-        k.wait()
-    for t in range(nb - 1):
-        for k in lines:
-            k.wait_send(t)
-
-
-def line_gather(arrays, nb):
-    na = len(arrays)
-    return pl.pallas_call(
-        functools.partial(line_kernel, nb, na),
-        out_shape=tuple(jax.ShapeDtypeStruct((nb,) + a.shape, a.dtype) for a in arrays),
-        in_specs=[VM] * na,
-        out_specs=(ANY,) * na,
-        scratch_shapes=[
-            pltpu.SemaphoreType.DMA((na, 2, nb - 1)),
-            pltpu.SemaphoreType.DMA((na, 2, nb - 1)),
-            pltpu.SemaphoreType.DMA((na,)),
-        ],
-        compiler_params=pltpu.CompilerParams(
-            collective_id=2, has_side_effects=True, vmem_limit_bytes=VMEM_LIMIT
-        ),
-        name="line_gather",
-    )(*arrays)
-
-
 def row_loop(rows, chunk, body):
     if rows == chunk:
         body(0)
@@ -255,9 +213,9 @@
 
 
 class PlaneReduce:
-    def __init__(self, p, nb, g, out, buf, ss, rs):
-        self.p, self.nb, self.g, self.out = p, nb, g, out
-        self.A, self.P, self.BX, self.BY, self.CX, self.CY, self.F, self.Z, self.O = buf
+    def __init__(self, p, nb, g, out, buf, ss, rs, ls):
+        self.p, self.nb, self.out = p, nb, out
+        self.G, self.P, self.BX, self.BY, self.CX, self.CY, self.Z, self.O = buf
         self.R, self.C = g.shape[-2:]
         self.dt = g.dtype
         self.ss, self.rs = ss, rs
@@ -266,11 +224,13 @@
         self.h = h
         lo, hi = pl.ds(0, h), pl.ds(h, h)
         self.chunk = 16 if C > 1024 else (48 if h % 48 == 0 else h)
-        self.cA = rcopy(g.at[:, :, 1 - p.c], self.A, ss.at[0], rs.at[0], p.C)
+        self.own = pltpu.make_async_copy(g.at[:, :, p.c], self.G, ls)
+        self.cA = rcopy(g.at[:, :, 1 - p.c], self.P, ss.at[0], rs.at[0], p.C)
         self.cBX = rcopy(self.P.at[:, 1 - p.x, lo], self.BX, ss.at[1], rs.at[1], p.X)
         self.cBY = rcopy(self.P.at[1 - p.s, :, hi], self.BY, ss.at[2], rs.at[2], p.Y)
         self.cCX = rcopy(self.P.at[p.s, 1 - p.x, hi], self.CX, ss.at[3], rs.at[3], p.X)
         self.cCY = rcopy(self.P.at[1 - p.s, p.x, lo], self.CY, ss.at[4], rs.at[4], p.Y)
+        self.F = self.P.at[p.s, p.x]
 
     def quarter(self, ref, j):
         R, C = self.R, self.C
@@ -282,19 +242,20 @@
 
     def a_start(self):
         self.cA.start()
+        self.own.start()
 
     def b_start(self):
+        self.own.wait()
         self.cA.wait_recv()
-        p, g, A, P, dt = self.p, self.g, self.A, self.P, self.dt
 
         def block(i, _):
             s, x = i // 2, i % 2
 
             def body(r):
                 rows = pl.ds(r, self.chunk)
-                P[s, x, rows] = (
-                    g[s, x, p.c, rows].astype(jnp.float32) + A[s, x, rows].astype(jnp.float32)
-                ).astype(dt)
+                self.P[s, x, rows] = (
+                    self.G[s, x, rows].astype(jnp.float32) + self.P[s, x, rows].astype(jnp.float32)
+                ).astype(self.dt)
             row_loop(self.R, self.chunk, body)
             return 0
         lax.fori_loop(0, 4, block, 0)
@@ -328,23 +289,11 @@
 
     def d_start(self):
         p, h, nb = self.p, self.h, self.nb
+        lo, hi = pl.ds(0, h), pl.ds(h, h)
         self.cCY.wait_recv()
+        self._add(self.F.at[lo], self.CY)
         self.cCX.wait_recv()
-
-        def lo_body(r):
-            rows = pl.ds(r, self.chunk)
-            self.F[rows] = (
-                self.P[p.s, p.x, rows].astype(jnp.float32) + self.CY[rows].astype(jnp.float32)
-            ).astype(self.dt)
-        row_loop(h, self.chunk, lo_body)
-
-        def hi_body(r):
-            rows = pl.ds(r + h, self.chunk)
-            self.F[rows] = (
-                self.P[p.s, p.x, rows].astype(jnp.float32)
-                + self.CX[pl.ds(r, self.chunk)].astype(jnp.float32)
-            ).astype(self.dt)
-        row_loop(h, self.chunk, hi_body)
+        self._add(self.F.at[hi], self.CX)
         for j in range(nb):
             @pl.when(p.b != j)
             def _():
@@ -403,7 +352,6 @@
         pltpu.VMEM((2, h, C), dt),
         pltpu.VMEM((h, C), dt),
         pltpu.VMEM((h, C), dt),
-        pltpu.VMEM((R, C), dt),
         pltpu.VMEM((nb, h, C // 2), dt),
         pltpu.VMEM((R, C), dt),
     ]
@@ -418,15 +366,25 @@
                 getattr(items[i], stages[k])()
 
 
+NBUF = 8
+
+
+def reducers(p, nb, nw, gs, outs, bufs, ss, rs, ls):
+    return [
+        PlaneReduce(
+            p, nb, gs[i], outs[i], bufs[NBUF * i:NBUF * (i + 1)], ss.at[i], rs.at[i], ls.at[i]
+        )
+        for i in range(nw)
+    ]
+
+
 def reduce_kernel(nb, nw, *refs):
     gs, outs = refs[:nw], refs[nw:2 * nw]
-    bufs = refs[2 * nw:2 * nw + 9 * nw]
-    ss, rs = refs[11 * nw:]
+    bufs = refs[2 * nw:(2 + NBUF) * nw]
+    ss, rs, ls = refs[(2 + NBUF) * nw:]
     p = Place()
     enter(p, nb, True, "all")
-    items = [
-        PlaneReduce(p, nb, gs[i], outs[i], bufs[9 * i:9 * i + 9], ss.at[i], rs.at[i]) for i in range(nw)
-    ]
+    items = reducers(p, nb, nw, gs, outs, bufs, ss, rs, ls)
     for k in items:
         k.a_start()
     wave(items, ("b_start", "c_start", "d_start", "e_start"))
@@ -445,9 +403,11 @@
     return pl.pallas_call(
         functools.partial(reduce_kernel, nb, nw),
         out_shape=tuple(jax.ShapeDtypeStruct(g.shape[-2:], jnp.float32) for g in grads),
-        in_specs=[VM] * nw,
+        in_specs=[ANY] * nw,
         out_specs=(VM,) * nw,
-        scratch_shapes=scratch + [pltpu.SemaphoreType.DMA((nw, ns)), pltpu.SemaphoreType.DMA((nw, ns))],
+        scratch_shapes=scratch + [
+            pltpu.SemaphoreType.DMA((nw, ns)), pltpu.SemaphoreType.DMA((nw, ns)), pltpu.SemaphoreType.DMA((nw,)),
+        ],
         compiler_params=pltpu.CompilerParams(
             collective_id=3, has_side_effects=True, vmem_limit_bytes=VMEM_LIMIT
         ),
@@ -458,7 +418,7 @@
 HEAD_DIM = 64
 PAIR = 128
 MASKED = -1e30
-TILE = 256
+TILE = 512
 
 
 def dot(a, b, ca, cb):
@@ -474,41 +434,53 @@
     return jnp.where(keep, pair, jnp.zeros_like(pair))
 
 
-def attn_fwd_kernel(span, col_ref, row_ref, q_ref, k_ref, v_ref, o_ref, ob_ref, lse_ref, m_ref, l_ref, acc_ref):
+def lane_groups(op, a):
+    out = a[:, :PAIR]
+    for g in range(1, a.shape[1] // PAIR):
+        out = op(out, a[:, g * PAIR:(g + 1) * PAIR])
+    return out
+
+
+def attn_fwd_kernel(span, col_ref, row_ref, q_ref, k_ref, v_ref, o_ref, ob_ref, lse_ref, s_ref, m_ref, l_ref, acc_ref):
     rows = q_ref.shape[0]
     left = left_lanes((rows, PAIR))
     m_ref[...] = jnp.full_like(m_ref, MASKED)
     l_ref[...] = jnp.zeros_like(l_ref)
     acc_ref[...] = jnp.zeros_like(acc_ref)
     q = q_ref[...]
-    heads = [one_head(q, left, True), one_head(q, left, False)]
+    heads = [one_head(q, left, i == 0) for i in range(2)]
     codes = col_ref[...]
 
-    def step(t, _):
+    def score(t, _):
         at = pl.multiple_of(t * TILE, TILE)
         k = k_ref[pl.ds(at, TILE), :]
-        v = v_ref[pl.ds(at, TILE), :]
         mask = codes == row_ref[:, pl.ds(at, TILE)]
-        alphas, parts = [], []
         for i in range(2):
             s = jnp.where(mask, dot(heads[i], k, 1, 1), MASKED)
-            old = m_ref[i]
-            new = jnp.maximum(old, jnp.max(s, axis=1, keepdims=True))
-            p = jnp.exp(s - new)
-            alpha = jnp.exp(old - new)
-            m_ref[i] = new
-            l_ref[i] = l_ref[i] * alpha + jnp.sum(p, axis=1, keepdims=True)
-            alphas.append(alpha)
+            s_ref[i, t] = s
+            m_ref[i] = jnp.maximum(m_ref[i], lane_groups(jnp.maximum, s))
+        return 0
+
+    lax.fori_loop(span[0], span[1], score, 0)
+    tops = [jnp.max(m_ref[i], axis=1, keepdims=True) for i in range(2)]
+
+    def mix(t, _):
+        v = v_ref[pl.ds(pl.multiple_of(t * TILE, TILE), TILE), :]
+        parts = []
+        for i in range(2):
+            p = jnp.exp(s_ref[i, t] - tops[i])
+            l_ref[i] += lane_groups(jnp.add, p)
             parts.append(dot(p.astype(jnp.bfloat16), v, 1, 0))
-        acc_ref[...] = acc_ref[...] * jnp.where(left, alphas[0], alphas[1]) + jnp.where(left, parts[0], parts[1])
+        acc_ref[...] += jnp.where(left, parts[0], parts[1])
         return 0
 
-    lax.fori_loop(span[0], span[1], step, 0)
-    total = jnp.where(left, l_ref[0], l_ref[1])
+    lax.fori_loop(span[0], span[1], mix, 0)
+    sums = [jnp.sum(l_ref[i], axis=1, keepdims=True) for i in range(2)]
+    total = jnp.where(left, sums[0], sums[1])
     o = acc_ref[...] / total
     o_ref[...] = o
     ob_ref[...] = o.astype(jnp.bfloat16)
-    lse_ref[...] = jnp.where(left, m_ref[0], m_ref[1]) + jnp.log(total)
+    lse_ref[...] = jnp.where(left, tops[0], tops[1]) + jnp.log(total)
 
 
 def attention(q, k_all, v_all, codes, own_codes, span):
@@ -529,8 +501,9 @@
             ],
             out_specs=[own, own, own],
             scratch_shapes=[
-                pltpu.VMEM((2, rows, 1), jnp.float32),
-                pltpu.VMEM((2, rows, 1), jnp.float32),
+                pltpu.VMEM((2, total // TILE, rows, TILE), jnp.float32),
+                pltpu.VMEM((2, rows, PAIR), jnp.float32),
+                pltpu.VMEM((2, rows, PAIR), jnp.float32),
                 pltpu.VMEM((rows, PAIR), jnp.float32),
             ],
         ),
@@ -575,7 +548,7 @@
 
 
 def attn_bwd_kernel(span, col_ref, row_ref, q_ref, k_ref, v_ref, g_ref, lse_ref, delta_ref,
-                    qa_ref, ka_ref, va_ref, ga_ref, st_ref, r_ref, rk_ref, rv_ref, dq_ref, dk_ref, dv_ref):
+                    qa_ref, ka_ref, va_ref, ga_ref, st_ref, dq_ref, dk_ref, dv_ref):
     rows = q_ref.shape[0]
     left = left_lanes((rows, PAIR))
     dq_ref[...] = jnp.zeros_like(dq_ref)
@@ -613,9 +586,6 @@
         return 0
 
     lax.fori_loop(span[0], span[1], step, 0)
-    r_ref[...] = dq_ref[...] * (HEAD_DIM ** (-0.5))
-    rk_ref[...] = dk_ref[...].astype(jnp.bfloat16)
-    rv_ref[...] = dv_ref[...]
 
 
 def attention_grad(q, k, v, g, lse, delta, q_all, k_all, v_all, g_all, stats, codes, own_codes, span):
@@ -636,16 +606,187 @@
                 pl.BlockSpec((1, 8, total), lambda h, s: (h, 0, 0)),
             ],
             out_specs=[own, own, own],
-            scratch_shapes=[pltpu.VMEM((rows, PAIR), jnp.float32)] * 3,
         ),
         out_shape=[
             jax.ShapeDtypeStruct((rows, width), jnp.float32),
-            jax.ShapeDtypeStruct((rows, width), jnp.bfloat16),
+            jax.ShapeDtypeStruct((rows, width), jnp.float32),
             jax.ShapeDtypeStruct((rows, width), jnp.float32),
         ],
         compiler_params=pltpu.CompilerParams(vmem_limit_bytes=48 << 20),
         name="attention_grad",
     )(span, own_codes.reshape(rows, 1), codes.reshape(1, total), q, k, v, g, lse, delta, q_all, k_all, v_all, g_all, stats)
+
+
+class AttentionGrad:
+    def __init__(self, codes, rows, q, k, v, g, lse, delta, stats, own, dq, dk, dv):
+        self.codes, self.rows = codes, rows
+        self.q, self.k, self.v, self.g = q, k, v, g
+        self.lse, self.delta, self.stats = lse, delta, stats
+        self.own = own
+        self.dq, self.dk, self.dv = dq, dk, dv
+        self.n = dq.shape[0]
+        self.pairs = dq.shape[1] // PAIR
+
+    def queries(self, j, first):
+        own = self.own
+
+        def pair(h, _):
+            left = left_lanes((self.n, PAIR))
+            lanes = pl.ds(pl.multiple_of(h * PAIR, PAIR), PAIR)
+            mask = self.codes[...] == self.rows[j]
+            q, g = self.q[own, :, lanes], self.g[own, :, lanes]
+            k, v = self.k[j, :, lanes], self.v[j, :, lanes]
+            lse, delta = self.lse[:, lanes], self.delta[:, lanes]
+            parts = []
+            for i in range(2):
+                at = slice(i * HEAD_DIM, i * HEAD_DIM + 1)
+                s = jnp.where(mask, dot(one_head(q, left, i == 0), k, 1, 1), MASKED)
+                p = jnp.exp(s - lse[:, at])
+                dp = dot(one_head(g, left, i == 0), v, 1, 1)
+                ds = (p * (dp - delta[:, at])).astype(jnp.bfloat16)
+                parts.append(dot(ds, k, 1, 0))
+            new = jnp.where(left, parts[0], parts[1])
+            if first:
+                self.dq[:, lanes] = new
+            else:
+                self.dq[:, lanes] += new
+            return 0
+
+        lax.fori_loop(0, self.pairs, pair, 0)
+
+    def keys(self, j, first):
+        own = self.own
+
+        def pair(h, _):
+            left = left_lanes((self.n, PAIR))
+            lanes = pl.ds(pl.multiple_of(h * PAIR, PAIR), PAIR)
+            mask = self.codes[...] == self.rows[j]
+            k, v = self.k[own, :, lanes], self.v[own, :, lanes]
+            q, g = self.q[j, :, lanes], self.g[j, :, lanes]
+            dks, dvs = [], []
+            for i in range(2):
+                st = jnp.where(mask, dot(one_head(k, left, i == 0), q, 1, 1), MASKED)
+                pt = jnp.exp(st - self.stats[j, h, i:i + 1])
+                dvs.append(dot(pt.astype(jnp.bfloat16), g, 1, 0))
+                dpt = dot(one_head(v, left, i == 0), g, 1, 1)
+                dst = (pt * (dpt - self.stats[j, h, 2 + i:3 + i])).astype(jnp.bfloat16)
+                dks.append(dot(dst, q, 1, 0))
+            dk, dv = jnp.where(left, dks[0], dks[1]), jnp.where(left, dvs[0], dvs[1])
+            if first:
+                self.dk[:, lanes] = dk
+                self.dv[:, lanes] = dv
+            else:
+                self.dk[:, lanes] += dk
+                self.dv[:, lanes] += dv
+            return 0
+
+        lax.fori_loop(0, self.pairs, pair, 0)
+
+
+def backward_kernel(nb, nw, *refs):
+    codes, rows, g_own, st_own, lse, delta, q_hbm, k_hbm, v_hbm = refs[:9]
+    gs = refs[9:9 + nw]
+    dq, dk, dv = refs[9 + nw:12 + nw]
+    outs = refs[12 + nw:12 + 2 * nw]
+    rest = refs[12 + 2 * nw:]
+    q, k, v, g, stats, zs, zr, ls = rest[:8]
+    bufs = rest[8:8 + NBUF * nw]
+    ss, rs, rls = rest[8 + NBUF * nw:]
+    p = Place()
+    loads = [
+        pltpu.make_async_copy(a, b, ls.at[i])
+        for i, (a, b) in enumerate(((k_hbm, k), (v_hbm, v), (q_hbm, q), (g_own, g.at[p.b]), (st_own, stats.at[p.b])))
+    ]
+    for c in loads:
+        c.start()
+    enter(p, nb, True, "all")
+    lines = [
+        LineGather(p, nb, g_own, g, zs.at[0], zr.at[0]),
+        LineGather(p, nb, st_own, stats, zs.at[1], zr.at[1]),
+    ]
+    items = reducers(p, nb, nw, gs, outs, bufs, ss, rs, rls)
+    for c in lines:
+        c.start(0)
+    for c in items:
+        c.a_start()
+    work = AttentionGrad(codes, rows, q, k, v, g, lse, delta, stats, p.b, dq, dk, dv)
+    for c in loads:
+        c.wait()
+
+    def arrived(t):
+        @pl.when(p.b - 1 - t >= 0)
+        def _():
+            work.keys(jnp.maximum(p.b - 1 - t, 0), False)
+
+        @pl.when(p.b + 1 + t <= nb - 1)
+        def _():
+            work.keys(jnp.minimum(p.b + 1 + t, nb - 1), False)
+
+    work.queries(p.b, True)
+    items[0].b_start()
+    work.queries((p.b + 1) % nb, False)
+    for c in items[1:]:
+        c.b_start()
+    work.queries((p.b + 2) % nb, False)
+    for c in lines:
+        c.wait_recv(0)
+        c.start(1)
+    items[0].c_start()
+    work.queries((p.b + 3) % nb, False)
+    items[1].c_start()
+    work.keys(p.b, True)
+    for c in lines:
+        c.wait_recv(1)
+        c.start(2)
+    items[0].d_start()
+    arrived(0)
+    items[2].c_start()
+    items[1].d_start()
+    arrived(1)
+    items[2].d_start()
+    items[0].e_start()
+    for c in lines:
+        c.wait_recv(2)
+    items[1].e_start()
+    arrived(2)
+    items[2].e_start()
+    for c in items:
+        c.finish()
+    for t in range(nb - 1):
+        for c in lines:
+            c.wait_send(t)
+    for c in items:
+        c.drain()
+
+
+def backward(codes, own_codes, do, stats, lse, delta, q_all, k_all, v_all, grads, nb):
+    rows, width = do.shape
+    nw = len(grads)
+    scratch = []
+    for g in grads:
+        scratch += reduce_scratch(g.shape[-2:], g.dtype, nb)
+    ns = 5 + 2 * nb
+    block = jax.ShapeDtypeStruct((rows, width), jnp.float32)
+    every = pltpu.VMEM((nb, rows, width), jnp.bfloat16)
+    return pl.pallas_call(
+        functools.partial(backward_kernel, nb, nw),
+        out_shape=(block,) * 3 + tuple(jax.ShapeDtypeStruct(g.shape[-2:], jnp.float32) for g in grads),
+        in_specs=[VM, VM, VM, VM, VM, VM, ANY, ANY, ANY] + [ANY] * nw,
+        out_specs=(VM,) * (3 + nw),
+        scratch_shapes=[
+            every, every, every, every,
+            pltpu.VMEM((nb,) + stats.shape, jnp.float32),
+            pltpu.SemaphoreType.DMA((2, 2, nb - 1)),
+            pltpu.SemaphoreType.DMA((2, 2, nb - 1)),
+            pltpu.SemaphoreType.DMA((5,)),
+        ] + scratch + [
+            pltpu.SemaphoreType.DMA((nw, ns)), pltpu.SemaphoreType.DMA((nw, ns)), pltpu.SemaphoreType.DMA((nw,)),
+        ],
+        compiler_params=pltpu.CompilerParams(
+            collective_id=4, has_side_effects=True, vmem_limit_bytes=60 << 20
+        ),
+        name="backward",
+    )(own_codes.reshape(rows, 1), codes.reshape(nb, 1, rows), do, stats, lse, delta, q_all, k_all, v_all, *grads)
 
 
 EPSILON = 1e-06
@@ -698,10 +839,11 @@
 
 
 def gather_line(arrays):
-    nb = lax.axis_size("blk")
-    if not tuned_plane():
-        return [lax.all_gather(a, "blk", axis=0) for a in arrays]
-    return line_gather(arrays, nb)
+    return [lax.all_gather(a, "blk", axis=0) for a in arrays]
+
+
+def shards(g):
+    return g.astype(jnp.bfloat16).reshape(2, 2, 2, g.shape[0] // 8, g.shape[1])
 
 
 def reduce_grads(mats, vecs):
@@ -714,7 +856,7 @@
     rows = [v.shape[0] // 8 for v in vecs]
     packed = jnp.concatenate([v.reshape(8, -1) for v in vecs], axis=1)
     packed = jnp.pad(packed, ((0, 0), (0, 16 * 256 - packed.shape[1])))
-    args = [g.astype(jnp.bfloat16).reshape(2, 2, 2, g.shape[0] // 8, g.shape[1]) for g in mats]
+    args = [shards(g) for g in mats]
     out = reduce_all(args + [packed.reshape(2, 2, 2, 16, 256)], nb)
     flat = out[-1].reshape(-1)
     parts, at = [], 0
@@ -782,12 +924,22 @@
     do = times_transpose(first_grad_low, wo).astype(jnp.bfloat16)
 
     stats, delta = row_stats(do, summed, lse)
-    do_all, stats_all = gather_line([do, stats])
-    stats_all = jnp.transpose(stats_all, (1, 2, 0, 3)).reshape(stats.shape[0], 8, total)
-    r, rk, dv = attention_grad(
-        q, k, v, do, lse, delta, q_all, k_all, v_all, do_all.reshape(total, width), stats_all,
-        codes, own_codes, span,
-    )
+    if tuned_plane():
+        early = [shards(g) for g in (wdn_grad, wup_grad, wo_grad)]
+        dq, dk, dv, rdn, rup, ro = backward(
+            codes, own_codes, do, stats, lse, delta, *[a.reshape(nb, rows, width) for a in (q_all, k_all, v_all)],
+            early, nb,
+        )
+    else:
+        do_all, stats_all = gather_line([do, stats])
+        stats_all = jnp.transpose(stats_all, (1, 2, 0, 3)).reshape(stats.shape[0], 8, total)
+        dq, dk, dv = attention_grad(
+            q, k, v, do, lse, delta, q_all, k_all, v_all, do_all.reshape(total, width), stats_all,
+            codes, own_codes, span,
+        )
+        (rdn, rup, ro), _ = reduce_grads([wdn_grad, wup_grad, wo_grad], [])
+    r = dq * scale
+    rk = dk.astype(jnp.bfloat16)
     bq_grad = jnp.sum(r, axis=0)
     bv_grad = jnp.sum(dv, axis=0)
     rq = r.astype(jnp.bfloat16)
@@ -798,10 +950,10 @@
     token_grad = first_grad + times_transpose(rq, wq) + times_transpose(rk, wk) + times_transpose(rv, wv)
 
     big, small = reduce_grads(
-        [wdn_grad, wup_grad, wo_grad, wq_grad, wk_grad, wv_grad],
+        [wq_grad, wk_grad, wv_grad],
         [bq_grad, bv_grad, bo_grad, g1_grad, s1_grad, bup_grad, bdn_grad, g2_grad, s2_grad],
     )
-    rdn, rup, ro, rwq, rwk, rwv = big
+    rwq, rwk, rwv = big
     return (
         result.astype(jnp.bfloat16)[None], token_grad.astype(jnp.bfloat16)[None],
         rwq, rwk, rwv, ro, small[0], small[1], small[2], small[3], small[4],

time: 600 us -> 387 us (0.65)
  the two profiles are of different devices: /device:TPU:1 before, /device:TPU:0 now
where the time goes in v2:
time: 387 us; the launch traced here: 385 us
  Pallas kernels  266 us (69%)
  matrix products  80 us (21%)
  local copies, waits for them, and re-layouts  25.4 us (7%)
  other arithmetic  8.81 us (2%)
  between operations  4.62 us (1%)
    pallas_call x1, Pallas kernels, backward(): pl.pallas_call(functools.partial(backward_kernel, nb, nw), out_shape=(blo...  123 us
    pallas_call x1, Pallas kernels, gather_all(): pl.pallas_call(functools.partial(gather_kernel, nb, nw), out_shape=outs,...  67.2 us
    dot_general x6, matrix products, mm(): return jnp.dot(left, right, preferred_element_type=jnp.float32)  41.6 us
    pallas_call x1, Pallas kernels, reduce_all(): pl.pallas_call(functools.partial(reduce_kernel, nb, nw), out_shape=tuple(...  41.5 us
    dot_general x12, matrix products, dot(): lax.dot_general(a, b, (((ca,), (cb,)), ((), ())), preferred_element_type=...  38.4 us
    pallas_call x1, Pallas kernels, attention(): pl.pallas_call(attn_fwd_kernel, grid_spec=pltpu.PrefetchScalarGridSpec(nu...  28.2 us
    unnamed x79, local copies, waits for them, and re-layouts  15.3 us

profile of v2, /device:TPU:0, one launch (start us, length us, event | category | flops | bytes accessed | tf_op | source)
XLA Modules:
  0.0 384.6 jit_solution(15269190518281571301)
XLA Ops:
  0.7 6.1 %concatenate.6 = bf16[1152]{0:T(1024)(128)(2,1)S(1)} concatenate(bf16[96]{0:T(256)(128)(2,1)} %param.26, bf16[96]{0:T(256)(128)(2,1)} %param.27, bf16[96]{0:T(256)(128)(2,1)} %param.28, bf16[96]{0:T(256)(128)(2,1)} %param.29, bf16[96]{0:T(256)(128)(2,1)} %param.30, bf16[384]{0:T(512)(128)(2,1)} %param.32, bf16[96]{0:T(256)(128)(2,1)} %param.34, bf16[96]{0:T(256)(128)(2,1)} %param.35, ...), dimensions={0} | concatenate | bytes 4608 | tf_op jit(solution)/shard_map/concatenate | solution.py:830
  6.8 0.6 pad_bitcast_fusion.refs_1_
  7.4 67.2 %gather_all.1 = (bf16[4,512,768]{2,1,0:T(8,128)(2,1)}, bf16[8,32,128]{2,1,0:T(8,128)(2,1)}, bf16[8,96,768]{2,1,0:T(8,128)(2,1)}, bf16[8,96,768]{2,1,0:T(8,128)(2...) custom-call(bf16[512,768]{1,0:T(8,128)(2,1)} %bitcast.91, ...), custom_call_target="tpu_custom_call" | custom-call | tf_op jit(solution)/shard_map/gather_all/pallas_call | solution.py:186
  74.6 0.9 copy.42
  75.5 0.1 slice_convert_fusion.2
  75.8 0.6 constant_dynamic-slice_fusion.2
  76.4 1.9 convert_reduce_fusion.2
  81.6 0.1 pad_add_fusion.span
  81.7 0.1 dynamic-slice_select_fusion
  81.8 0.1 copy.36.col_ref.refs_0_
  82.1 5.0 %multiply_convert_fusion.1 = bf16[2048,768]{1,0:T(8,128)(2,1)S(1)} fusion(bf16[2048,768]{1,0:T(8,128)(2,1)} %bitcast.128, bf16[768,768]{1,0:T(8,128)(2,1)} %bitcast.103, f32[768]{0:T(1024)S(1)} %reshape.346), kind=kOutput, calls=%fused_computation.17 | convolution fusion | flops 2420637696 | bytes 7474176 | tf_op jit(solution)/shard_map/dot_general | solution.py:807
  87.2 2.1 copy-done.20
  89.2 4.5 %convolution_convert_fusion.2.k_ref = bf16[2048,768]{1,0:T(8,128)(2,1)} fusion(bf16[2048,768]{1,0:T(8,128)(2,1)S(1)} %bitcast.130, bf16[768,768]{1,0:T(8,128)(2,1)S(1)} %bitcast.105), kind=kOutput, calls=%fused_computation.21 | convolution fusion | flops 2417491968 | bytes 7471104 | tf_op jit(solution)/shard_map/dot_general | solution.py:807
  93.8 6.3 %add_convert_fusion.v_ref = bf16[2048,768]{1,0:T(8,128)(2,1)} fusion(bf16[2048,768]{1,0:T(8,128)(2,1)} %bitcast.129, bf16[768,768]{1,0:T(8,128)(2,1)S(1)} %bitcast.100, f32[768]{0:T(1024)S(1)} %reshape.347), kind=kOutput, calls=%fused_computation.16 | convolution fusion | flops 2419064832 | bytes 7474176 | tf_op jit(solution)/shard_map/dot_general | solution.py:807
  100.1 28.2 %attention.1 = (f32[512,768]{1,0:T(8,128)S(1)}, bf16[512,768]{1,0:T(8,128)(2,1)S(1)}, f32[512,768]{1,0:T(8,128)S(1)}) custom-call(s32[2]{0:T(128)S(1)} %pad_add_fusion.span, s32[512,1]{1,0:T(8,128)S(1)} %copy.36.col_ref.refs_0_, s32[1,2048]{1,0:T(1,128)S(1)} %subtract_select_fusion.2.row_ref, bf16[512,768]{1,0:T(8,128)(2,1)S(1)} %constant_dynamic-slice_fusion.1.q_ref, ...), custom_call_target="tpu_custom_call" | custom-call | tf_op jit(solution)/shard_map/attention/pallas_call | solution.py:492
  128.3 0.9 fusion.43
  129.2 0.3 copy-done
  129.4 0.4 copy-done.2
  130.0 0.3 multiply_reduce_fusion.3
  130.4 19.7 %multiply_convert_fusion = (bf16[512,3072]{1,0:T(8,128)(2,1)S(1)}, f32[512,3072]{1,0:T(8,128)}, f32[512,3072]{1,0:T(8,128)}) fusion(f32[3072]{0:T(1024)S(1)} %reshape.351, bf16[768,3072]{1,0:T(8,128)(2,1)} %bitcast.120, f32[512,768]{1,0:T(8,128)S(1)} %get-tuple-element.98, f32[768]{0:T(1024)S(1)} %reshape.350, f32[768]{0:T(1024)S(1)} %reshape.349, ...), kind=kOutput, calls=%fused_computation.3 | convolution fusion | flops 2521694208 | bytes 22042624 | tf_op jit(solution)/shard_map/dot_general | solution.py:807
  150.1 5.3 %fusion.44 = (f32[512]{0:T(512)S(1)}, f32[512,768]{1,0:T(8,128)S(1)}) fusion(f32[768]{0:T(1024)S(1)} %reshape.352, bf16[512,3072]{1,0:T(8,128)(2,1)S(1)} %get-tuple-element.74, bf16[3072,768]{1,0:T(8,128)(2,1)S(1)} %bitcast.127, f32[768]{0:T(1024)S(1)} %reshape.350, f32[768]{0:T(1024)S(1)} %reshape.349, f32[512]{0:T(512)S(1)} %fusion.27, ...), kind=kOutput, calls=%fused_computation.109 | convolution fusion | flops 2418671104 | bytes 11025408 | tf_op jit(solution)/shard_map/dot_general | solution.py:807
  155.5 0.3 multiply_reduce_fusion.2
  155.9 0.7 copy-done.7
  156.6 0.8 fusion.11
  157.4 1.6 fusion.40
  159.0 0.7 subtract_select_fusion.1.refs_1_
  159.7 8.7 %fusion.45 = (f32[3072]{0:T(1024)S(1)}, bf16[512,3072]{1,0:T(8,128)(2,1)S(1)}) fusion(f32[512,3072]{1,0:T(8,128)} %get-tuple-element.75, bf16[3072,768]{1,0:T(8,128)(2,1)} %bitcast.124, f32[512,768]{1,0:T(8,128)S(1)} %get-tuple-element.73, f32[512]{0:T(512)S(1)} %negate_multiply_fusion.2, f32[512,3072]{1,0:T(8,128)} %get-tuple-element.99, ...), kind=kOutput, calls=%fused_computation.110 | convolution fusion | flops 2441868288 | bytes 22046720 | tf_op jit(solution)/shard_map/dot_general | solution.py:425
  168.5 3.2 multiply_reduce_fusion
  171.7 0.6 fusion.39
  172.3 0.6 copy-done.27
  172.9 1.7 convolution_convert_fusion.7.g_ref.refs_2_
  174.7 6.1 %row_stats.1 = (f32[6,8,512]{2,1,0:T(8,128)}, f32[512,768]{1,0:T(8,128)}) custom-call(bf16[512,768]{1,0:T(8,128)(2,1)} %convolution_convert_fusion.7.g_ref.refs_2_, f32[512,768]{1,0:T(8,128)} %copy-done.2, f32[512,768]{1,0:T(8,128)} %copy-done), custom_call_target="tpu_custom_call" | custom-call | tf_op jit(solution)/shard_map/row_stats/pallas_call | solution.py:537
  180.8 7.4 %convolution_convert_fusion.1 = bf16[3072,768]{1,0:T(8,128)(2,1)} fusion(bf16[512,3072]{1,0:T(8,128)(2,1)} %copy-done.30, f32[512,768]{1,0:T(8,128)} %copy-done.10, f32[512]{0:T(512)S(1)} %negate_multiply_fusion.2), kind=kOutput, calls=%fused_computation.20 | convolution fusion | flops 2419064832 | bytes 9439232 | tf_op jit(solution)/shard_map/dot_general | solution.py:425
  188.2 4.9 %convolution_convert_fusion = bf16[768,3072]{1,0:T(8,128)(2,1)} fusion(bf16[512,3072]{1,0:T(8,128)(2,1)S(1)} %copy-done.29, f32[512,768]{1,0:T(8,128)S(1)} %copy-done.13, f32[768]{0:T(1024)S(1)} %reshape.350, f32[768]{0:T(1024)S(1)} %reshape.349, f32[512]{0:T(512)S(1)} %fusion.27, f32[512]{0:T(512)S(1)} %broadcast_multiply_fusion.1), kind=kOutput, calls=%fused_computation.19 | convolution fusion | flops 2420244480 | bytes 9447424 | tf_op jit(solution)/shard_map/dot_general | solution.py:425
  193.1 1.9 convolution_convert_fusion.6
  195.0 122.7 %backward.1 = (f32[512,768]{1,0:T(8,128)}, f32[512,768]{1,0:T(8,128)}, f32[512,768]{1,0:T(8,128)}, f32[384,768]{1,0:T(8,128)}, f32[96,3072]{1,0:T(8,128)}, /*index=5*/f32[96,768]{1,0:T(8,128)}) custom-call(s32[512,1]{1,0:T(8,128)} %copy-done.1, s32[4,1,512]{2,1,0:T(1,128)} %subtract_select_fusion.1.refs_1_, ...), custom_call_target="tpu_custom_call" | custom-call | tf_op jit(solution)/shard_map/backward/pallas_call | solution.py:771
  317.8 2.4 fusion.24
  320.2 0.8 fusion.26
  321.0 0.5 copy-done.3
  321.6 0.3 copy-done.16
  321.9 1.8 fusion.18
  323.7 1.8 convolution_convert_fusion.5
  325.6 1.9 convolution_convert_fusion.4
  327.4 1.8 convolution_convert_fusion.3
  329.3 0.1 multiply_reduce_fusion.4
  329.4 0.1 reshape.335
  329.5 0.1 reduce_sum.184
  329.6 0.1 reshape.336
  329.7 0.2 add_reduce_fusion
  330.1 1.6 add_reduce_fusion.1
  331.9 0.1 convert_reduce_fusion
  332.0 0.1 reshape.343
  332.1 0.1 concatenate.7
  332.2 0.7 copy.39
  332.9 41.5 %reduce_all.1 = (f32[96,768]{1,0:T(8,128)}, f32[96,768]{1,0:T(8,128)}, f32[96,768]{1,0:T(8,128)}, f32[16,256]{1,0:T(8,128)}) custom-call(bf16[2,2,2,96,768]{4,3,2,1,0:T(8,128)(2,1)} %bitcast.95, bf16[2,2,2,96,768]{4,3,2,1,0:T(8,128)(2,1)} %bitcast.96, bf16[2,2,2,96,768]{4,3,2,1,0:T(8,128)(2,1)} %bitcast.97, f32[2,2,2,16,256]{4,3,2,1,0:T(8,128)} %bitcast.107), custom_call_target="tpu_custom_call" | custom-call | tf_op jit(solution)/shard_map/reduce_all/pallas_call | solution.py:403
  374.5 0.8 copy.40
  375.3 0.6 fusion.42
  375.9 0.6 slice.96
  376.6 1.7 copy.49
  378.3 1.7 copy.50
  380.0 1.7 copy.51
  381.7 0.7 copy.52
  382.4 1.0 copy.53
  383.4 1.0 copy.54
  (93 shorter events, 1.3 us)
Async XLA Ops:
  0.7 75.1 %copy-start.23 = (s32[1,2048]{1,0:T(1,128)S(1)}, s32[1,2048]{1,0:T(1,128)}, u32[]{:S(2)}) copy-start(s32[1,2048]{1,0:T(1,128)} %param.20) | copy-start | bytes 24580
  0.7 81.0 %copy-start.24 = (s32[1,2048]{1,0:T(1,128)S(1)}, s32[1,2048]{1,0:T(1,128)}, u32[]{:S(2)}) copy-start(s32[1,2048]{1,0:T(1,128)} %param.21) | copy-start | bytes 24580
  82.0 18.1 %copy-start.1 = (s32[512,1]{1,0:T(8,128)}, s32[512,1]{1,0:T(8,128)S(1)}, u32[]{:S(2)}) copy-start(s32[512,1]{1,0:T(8,128)S(1)} %copy.36.col_ref.refs_0_) | copy-start | bytes 6148
  82.1 5.1 %copy-start.25 = (bf16[4,512,768]{2,1,0:T(8,128)(2,1)S(1)}, bf16[4,512,768]{2,1,0:T(8,128)(2,1)}, u32[]{:S(2)}) copy-start(bf16[4,512,768]{2,1,0:T(8,128)(2,1)} %get-tuple-element.40) | copy-start | bytes 9437188
  87.1 6.6 %copy-start.14 = (bf16[2048,768]{1,0:T(8,128)(2,1)}, bf16[2048,768]{1,0:T(8,128)(2,1)S(1)}, u32[]{:S(2)}) copy-start(bf16[2048,768]{1,0:T(8,128)(2,1)S(1)} %multiply_convert_fusion.1) | copy-start | bytes 9437188
  87.1 2.1 copy-start.20
  89.2 4.5 %copy-start.15 = (bf16[8,96,768]{2,1,0:T(8,128)(2,1)S(1)}, bf16[8,96,768]{2,1,0:T(8,128)(2,1)}, u32[]{:S(2)}) copy-start(bf16[8,96,768]{2,1,0:T(8,128)(2,1)} %get-tuple-element.44) | copy-start | bytes 3538948
  100.0 28.2 %copy-start.5 = (bf16[1,512,768]{2,1,0:T(8,128)(2,1)S(1)}, bf16[1,512,768]{2,1,0:T(8,128)(2,1)}, u32[]{:S(2)}) copy-start(bf16[1,512,768]{2,1,0:T(8,128)(2,1)} %param.19) | copy-start | bytes 2359300
  100.1 28.2 %copy-start.26 = (bf16[8,96,768]{2,1,0:T(8,128)(2,1)S(1)}, bf16[8,96,768]{2,1,0:T(8,128)(2,1)}, u32[]{:S(2)}) copy-start(bf16[8,96,768]{2,1,0:T(8,128)(2,1)} %get-tuple-element.46) | copy-start | bytes 3538948
  128.3 1.2 copy-start
  128.3 1.6 copy-start.2
  128.3 21.8 %slice-start.2 = ((s8[4718592]{0:T(1024)(128)(4,1)}), s8[524288]{0:T(1024)(128)(4,1)S(1)}, s32[]{:S(2)}) async-start(s8[4718592]{0:T(1024)(128)(4,1)} %bitcast.125), calls=%async_computation.2 | async-start | bytes 1048576
  129.9 20.2 %copy-start.11 = (f32[512,768]{1,0:T(8,128)}, f32[512,768]{1,0:T(8,128)S(1)}, u32[]{:S(2)}) copy-start(f32[512,768]{1,0:T(8,128)S(1)} %get-tuple-element.98) | copy-start | bytes 4718596
  130.3 19.8 %slice-start.3 = ((s8[4718592]{0:T(1024)(128)(4,1)}), s8[4194304]{0:T(1024)(128)(4,1)S(1)}, s32[]{:S(2)}) async-start(s8[4718592]{0:T(1024)(128)(4,1)} %bitcast.125), calls=%async_computation.3 | async-start | bytes 8388608
  150.1 5.3 %copy-start.30 = (bf16[512,3072]{1,0:T(8,128)(2,1)}, bf16[512,3072]{1,0:T(8,128)(2,1)S(1)}, u32[]{:S(2)}) copy-start(bf16[512,3072]{1,0:T(8,128)(2,1)S(1)} %get-tuple-element.74) | copy-start | bytes 9437188
  155.4 1.1 copy-start.7
  157.4 11.0 %slice-start = ((s8[4718592]{0:T(1024)(128)(4,1)}), s8[4194304]{0:T(1024)(128)(4,1)S(1)}, s32[]{:S(2)}) async-start(s8[4718592]{0:T(1024)(128)(4,1)} %bitcast.121), calls=%async_computation | async-start | bytes 8388608
  159.0 9.4 %copy-start.10 = (f32[512,768]{1,0:T(8,128)}, f32[512,768]{1,0:T(8,128)S(1)}, u32[]{:S(2)}) copy-start(f32[512,768]{1,0:T(8,128)S(1)} %get-tuple-element.73) | copy-start | bytes 4718596
  159.7 8.8 %copy-start.12 = (f32[512,768]{1,0:T(8,128)S(1)}, f32[512,768]{1,0:T(8,128)}, u32[]{:S(2)}) copy-start(f32[512,768]{1,0:T(8,128)} %copy-done.11) | copy-start | bytes 4718596
  159.7 8.8 %slice-start.1 = ((s8[4718592]{0:T(1024)(128)(4,1)}), s8[524288]{0:T(1024)(128)(4,1)S(1)}, s32[]{:S(2)}) async-start(s8[4718592]{0:T(1024)(128)(4,1)} %bitcast.121), calls=%async_computation.1 | async-start | bytes 1048576
  168.4 3.2 copy-start.28
  171.7 1.3 copy-start.27
  180.8 7.4 %copy-start.13 = (f32[512,768]{1,0:T(8,128)S(1)}, f32[512,768]{1,0:T(8,128)}, u32[]{:S(2)}) copy-start(f32[512,768]{1,0:T(8,128)} %copy-done.11) | copy-start | bytes 4718596
  180.8 7.4 %copy-start.29 = (bf16[512,3072]{1,0:T(8,128)(2,1)S(1)}, bf16[512,3072]{1,0:T(8,128)(2,1)}, u32[]{:S(2)}) copy-start(bf16[512,3072]{1,0:T(8,128)(2,1)} %copy-done.28) | copy-start | bytes 9437188
  195.0 122.8 %copy-start.21 = (bf16[8,96,768]{2,1,0:T(8,128)(2,1)S(1)}, bf16[8,96,768]{2,1,0:T(8,128)(2,1)}, u32[]{:S(2)}) copy-start(bf16[8,96,768]{2,1,0:T(8,128)(2,1)} %get-tuple-element.43) | copy-start | bytes 3538948
  317.7 2.4 copy-start.4
  317.7 2.4 copy-start.19
  320.2 1.4 copy-start.3
  320.2 1.7 copy-start.16
  321.9 1.8 copy-start.6
  323.7 1.9 copy-start.9
  329.7 2.1 copy-start.8
  374.4 7.2 %copy-start.22 = (f32[96,768]{1,0:T(8,128)S(1)}, f32[96,768]{1,0:T(8,128)}, u32[]{:S(2)}) copy-start(f32[96,768]{1,0:T(8,128)} %get-tuple-element.129) | copy-start | bytes 884740
  374.5 7.9 %copy-start.18 = (f32[96,3072]{1,0:T(8,128)S(1)}, f32[96,3072]{1,0:T(8,128)}, u32[]{:S(2)}) copy-start(f32[96,3072]{1,0:T(8,128)} %get-tuple-element.135) | copy-start | bytes 3538948
  381.7 1.7 copy-start.17
